TPU v7x, 32 devices: a whole 2x2x4 slice. The times are simulated.
32 devices in a mesh: wide: 8 (over z, x), narrow: 4 (over y, core).
Axes of the slice: x: 2, y: 2, z: 4, core: 2. Of those that a mesh axis runs over, the one named last changes fastest.
Arguments:
- patches: bfloat16 [4096, 256], P(('wide', 'narrow')), may hold values from -6 to 6
- token_kind: int32 [4096], P(('wide', 'narrow')), may hold values 0 or 1
- mask_slots: int32 [16, 64], P('wide'), may hold values from 0 to 255
- projector: bfloat16 [2, 256, 768], replicated, may hold values from -0.375 to 0.375
- offsets: bfloat16 [2, 768], replicated, may hold values from -3 to 3
- placeholder: bfloat16 [768], replicated, may hold values from -4 to 4
- positions: bfloat16 [256, 768], replicated, may hold values from -3 to 3
- scales: bfloat16 [2, 2, 768], replicated, may hold values from 0.5 to 1.5
- shifts: bfloat16 [2, 2, 768], replicated, may hold values from -3 to 3
- attention: bfloat16 [2, 3, 768, 768], P(None, None, None, 'narrow'), may hold values from -0.21875 to 0.21875
- attn_bias: bfloat16 [2, 2, 768], P(None, None, 'narrow'), may hold values from -3 to 3
- combiner: bfloat16 [2, 768, 768], P(None, 'narrow'), may hold values from -1.75 to 1.75
- comb_bias: bfloat16 [2, 768], replicated, may hold values from -3 to 3
- expander: bfloat16 [2, 768, 3072], P(None, None, 'narrow'), may hold values from -0.21875 to 0.21875
- expand_bias: bfloat16 [2, 3072], P(None, 'narrow'), may hold values from -3 to 3
- reducer: bfloat16 [2, 3072, 768], P(None, 'narrow'), may hold values from -0.15625 to 0.15625
- reduce_bias: bfloat16 [2, 768], replicated, may hold values from -3 to 3
- cotangent: bfloat16 [4096, 768], P(('wide', 'narrow')), may hold values from -6 to 6
Outputs:
- encoded: float32 [4096, 768], P(('wide', 'narrow'))
- grad_patches: float32 [4096, 256], P(('wide', 'narrow'))
- grad_projector: float32 [2, 256, 768], replicated
- grad_offsets: float32 [2, 768], replicated
- grad_placeholder: float32 [768], replicated
- grad_positions: float32 [256, 768], replicated
- grad_scales: float32 [2, 2, 768], replicated
- grad_shifts: float32 [2, 2, 768], replicated
- grad_attention: float32 [2, 3, 768, 768], P(None, None, None, 'narrow')
- grad_attnbias: float32 [2, 2, 768], P(None, None, 'narrow')
- grad_combiner: float32 [2, 768, 768], P(None, 'narrow')
- grad_combbias: float32 [2, 768], replicated
- grad_expander: float32 [2, 768, 3072], P(None, None, 'narrow')
- grad_expbias: float32 [2, 3072], P(None, 'narrow')
- grad_reducer: float32 [2, 3072, 768], P(None, 'narrow')
- grad_redbias: float32 [2, 768], replicated
Inputs may be any that keep to these rules, and one draw needn't show every extreme that they name: `mask_slots`: positions within the clip; a position may appear more than once.
All inputs are finite; a program needn't handle non-finite values. No bound on the sum of `token_kind` on one device may be relied on, other than what follows from the above.
Results may differ from a plain program's by a relative error of at most 0.025.
Values may be sent and summed in bfloat16 or wider, within the bound.
A program may use at most 128 MiB of HBM per device.

v0:
```python
from functools import partial
import math

import jax
import jax.numpy as jnp
from jax import lax
from jax.sharding import PartitionSpec as P

HD = 64


norm_eps = 1e-06


def normalize(values, gain, shift):
    center = values - jnp.mean(values, axis=-1, keepdims=True)
    variance = jnp.mean(center * center, axis=-1, keepdims=True)
    return center * lax.rsqrt(variance + norm_eps) * gain + shift


def norm_params(values, grad):
    center = values - jnp.mean(values, axis=-1, keepdims=True)
    variance = jnp.mean(center * center, axis=-1, keepdims=True)
    hat = center * lax.rsqrt(variance + norm_eps)
    return (jnp.sum(grad * hat, axis=0), jnp.sum(grad, axis=0))


def share_rows(values):
    return lax.all_gather(values, "narrow", axis=0, tiled=True)


def share_grads(values):
    return lax.all_gather(values, "narrow", axis=0, tiled=True)


def sum_forward(source, weight, local_rows):

    def term(start, count):
        return jnp.dot(source, weight, preferred_element_type=jnp.float32)

    return lax.psum_scatter(
        term(jnp.int32(0), local_rows * lax.axis_size("narrow")).astype(jnp.bfloat16),
        "narrow",
        scatter_dimension=0,
        tiled=True,
    ).astype(jnp.float32)


def sum_backward(source, weight, local_rows):

    def term(start, count):
        return jnp.einsum("rk,dk->rd", source, weight, preferred_element_type=jnp.float32)

    return lax.psum_scatter(
        term(jnp.int32(0), local_rows * lax.axis_size("narrow")).astype(jnp.bfloat16),
        "narrow",
        scatter_dimension=0,
        tiled=True,
    ).astype(jnp.float32)


def attend_block(inputs):
    query, key, value = inputs
    scores = jnp.einsum("bqhd,bkhd->bhqk", query, key, preferred_element_type=jnp.float32)
    top = jnp.max(scores, axis=-1, keepdims=True)
    raised = jnp.exp(scores - top)
    total = jnp.sum(raised, axis=-1, keepdims=True)
    weights = raised / total
    mixed = jnp.einsum(
        "bhqk,bkhd->bqhd", weights.astype(jnp.bfloat16), value, preferred_element_type=jnp.float32
    )
    return (mixed.astype(jnp.bfloat16), top + jnp.log(total))


def attend_back(inputs):
    query, key, value, log_total, grad_mixed = inputs
    scores = jnp.einsum("bqhd,bkhd->bhqk", query, key, preferred_element_type=jnp.float32)
    weights = jnp.exp(scores - log_total)
    grad_weights = jnp.einsum(
        "bqhd,bkhd->bhqk", grad_mixed, value, preferred_element_type=jnp.float32
    )
    grad_value = jnp.einsum(
        "bhqk,bqhd->bkhd",
        weights.astype(jnp.bfloat16),
        grad_mixed,
        preferred_element_type=jnp.float32,
    ).astype(jnp.bfloat16)
    center = jnp.sum(weights * grad_weights, axis=-1, keepdims=True)
    grad_scores = (weights * (grad_weights - center)).astype(jnp.bfloat16)
    grad_query = jnp.einsum(
        "bhqk,bkhd->bqhd", grad_scores, key, preferred_element_type=jnp.float32
    ).astype(jnp.bfloat16)
    grad_key = jnp.einsum(
        "bhqk,bqhd->bkhd", grad_scores, query, preferred_element_type=jnp.float32
    ).astype(jnp.bfloat16)
    return (grad_query, grad_key, grad_value)


def per_device(
    patches,
    token_kind,
    mask_slots,
    projector,
    offsets,
    placeholder,
    positions,
    scales,
    shifts,
    attention,
    attn_bias,
    combiner,
    comb_bias,
    expander,
    expand_bias,
    reducer,
    reduce_bias,
    cotangent,
):
    local_rows, patch_len = patches.shape
    width = projector.shape[2]
    clip_count = mask_slots.shape[0]
    seq_len = positions.shape[0]
    group_rows = clip_count * seq_len
    start_row = lax.axis_index("narrow") * local_rows
    head_cols = attention.shape[3]
    local_heads = head_cols // HD
    layer_count = scales.shape[0]
    scale = HD ** (-0.5)
    block_clips = math.gcd(clip_count, max(1, 512 // seq_len))
    block_count = clip_count // block_clips
    head_shape = (block_count, block_clips, seq_len, local_heads, HD)
    place = jnp.arange(seq_len, dtype=jnp.int32)
    masked_group = jnp.any(mask_slots[:, :, None] == place[None, None, :], axis=1).reshape(
        group_rows, 1
    )
    masked = lax.dynamic_slice_in_dim(masked_group, start_row, local_rows, 0)
    is_patch = (token_kind == 1).reshape(local_rows, 1)
    blank = jnp.zeros_like(patches)
    widened = jnp.concatenate(
        [jnp.where(is_patch, blank, patches), jnp.where(is_patch, patches, blank)], axis=1
    )
    flat_projector = projector.reshape(2 * patch_len, width)
    lifted = jnp.dot(widened, flat_projector, preferred_element_type=jnp.float32)
    shifted = lifted + jnp.where(
        is_patch, offsets[1].astype(jnp.float32), offsets[0].astype(jnp.float32)
    )
    table = jnp.broadcast_to(positions.astype(jnp.float32)[None], (clip_count, seq_len, width))
    position_rows = lax.dynamic_slice_in_dim(
        table.reshape(group_rows, width), start_row, local_rows, 0
    )
    stream = jnp.where(masked, placeholder.astype(jnp.float32), shifted) + position_rows
    grad_top = cotangent.astype(jnp.float32)
    saved = []
    for layer in range(layer_count):
        first = normalize(
            stream, scales[layer, 0].astype(jnp.float32), shifts[layer, 0].astype(jnp.float32)
        ).astype(jnp.bfloat16)
        first_all = share_rows(first)
        joined = attention[layer].transpose(1, 0, 2).reshape(width, 3 * head_cols)
        triple = jnp.dot(first_all, joined, preferred_element_type=jnp.float32)
        query = ((triple[:, :head_cols] + attn_bias[layer, 0].astype(jnp.float32)) * scale).astype(
            jnp.bfloat16
        )
        key = triple[:, head_cols : 2 * head_cols].astype(jnp.bfloat16)
        value = (triple[:, 2 * head_cols :] + attn_bias[layer, 1].astype(jnp.float32)).astype(
            jnp.bfloat16
        )
        mixed, log_total = lax.map(
            attend_block,
            (query.reshape(head_shape), key.reshape(head_shape), value.reshape(head_shape)),
        )
        mixed = mixed.reshape(group_rows, head_cols)
        middle = (
            stream
            + sum_forward(mixed, combiner[layer], local_rows)
            + comb_bias[layer].astype(jnp.float32)
        )
        second = normalize(
            middle, scales[layer, 1].astype(jnp.float32), shifts[layer, 1].astype(jnp.float32)
        ).astype(jnp.bfloat16)
        second_all = share_rows(second)
        pre_act = jnp.dot(
            second_all, expander[layer], preferred_element_type=jnp.float32
        ) + expand_bias[layer].astype(jnp.float32)
        hidden = jax.nn.gelu(pre_act, approximate=False).astype(jnp.bfloat16)
        saved.append(
            (
                stream,
                first_all,
                query,
                key,
                value,
                log_total,
                mixed,
                middle,
                second_all,
                pre_act,
                hidden,
            )
        )
        stream = (
            middle
            + sum_forward(hidden, reducer[layer], local_rows)
            + reduce_bias[layer].astype(jnp.float32)
        )
    grad_stream = grad_top
    owned = [None] * layer_count
    gain_grads = [None] * layer_count
    shift_grads = [None] * layer_count
    comb_grads = [None] * layer_count
    red_grads = [None] * layer_count
    for layer in reversed(range(layer_count)):
        (
            stream_in,
            first_all,
            query,
            key,
            value,
            log_total,
            mixed,
            middle,
            second_all,
            pre_act,
            hidden,
        ) = saved[layer]
        red_grads[layer] = jnp.sum(grad_stream, axis=0)
        out_round = share_grads(grad_stream.astype(jnp.bfloat16))
        grad_reducer = jnp.einsum(
            "rf,rd->fd", hidden, out_round, preferred_element_type=jnp.float32
        )
        grad_hidden = jnp.einsum(
            "rd,fd->rf", out_round, reducer[layer], preferred_element_type=jnp.float32
        )
        _, gelu_back = jax.vjp(partial(jax.nn.gelu, approximate=False), pre_act)
        grad_pre = gelu_back(grad_hidden)[0]
        grad_expbias = jnp.sum(grad_pre, axis=0)
        pre_round = grad_pre.astype(jnp.bfloat16)
        grad_expander = jnp.einsum(
            "rd,rf->df", second_all, pre_round, preferred_element_type=jnp.float32
        )
        grad_second = sum_backward(pre_round, expander[layer], local_rows)
        _, norm_back = jax.vjp(
            normalize,
            middle,
            scales[layer, 1].astype(jnp.float32),
            shifts[layer, 1].astype(jnp.float32),
        )
        grad_mid_in = norm_back(grad_second)[0]
        grad_gain_two, grad_shift_two = norm_params(middle, grad_second)
        grad_middle = grad_stream + grad_mid_in
        comb_grads[layer] = jnp.sum(grad_middle, axis=0)
        mid_round = share_grads(grad_middle.astype(jnp.bfloat16))
        grad_combiner = jnp.einsum(
            "re,rd->ed", mixed, mid_round, preferred_element_type=jnp.float32
        )
        grad_mixed = jnp.einsum(
            "rd,ed->re", mid_round, combiner[layer], preferred_element_type=jnp.float32
        ).astype(jnp.bfloat16)
        grad_query, grad_key, grad_value = lax.map(
            attend_back,
            (
                query.reshape(head_shape),
                key.reshape(head_shape),
                value.reshape(head_shape),
                log_total,
                grad_mixed.reshape(head_shape),
            ),
        )
        grad_query = grad_query.reshape(group_rows, head_cols) * scale
        grad_value = grad_value.reshape(group_rows, head_cols)
        grad_triple = jnp.concatenate(
            [grad_query, grad_key.reshape(group_rows, head_cols), grad_value], axis=1
        )
        grad_joined = jnp.einsum(
            "rd,rk->dk", first_all, grad_triple, preferred_element_type=jnp.float32
        )
        grad_attention = grad_joined.reshape(width, 3, head_cols).transpose(1, 0, 2)
        grad_attnbias = jnp.stack(
            [
                jnp.sum(grad_query.astype(jnp.float32), axis=0),
                jnp.sum(grad_value.astype(jnp.float32), axis=0),
            ]
        )
        joined = attention[layer].transpose(1, 0, 2).reshape(width, 3 * head_cols)
        grad_first = sum_backward(grad_triple, joined, local_rows)
        _, norm_back = jax.vjp(
            normalize,
            stream_in,
            scales[layer, 0].astype(jnp.float32),
            shifts[layer, 0].astype(jnp.float32),
        )
        grad_in = norm_back(grad_first)[0]
        grad_gain_one, grad_shift_one = norm_params(stream_in, grad_first)
        grad_stream = grad_middle + grad_in
        gain_grads[layer] = jnp.stack([grad_gain_one, grad_gain_two])
        shift_grads[layer] = jnp.stack([grad_shift_one, grad_shift_two])
        own_grads = (
            grad_attention,
            grad_attnbias,
            grad_combiner,
            grad_expander,
            grad_expbias,
            grad_reducer,
        )
        own_grads = lax.psum(
            (
                grad_attention,
                grad_attnbias,
                grad_combiner,
                grad_expander,
                grad_expbias,
                grad_reducer,
            ),
            "wide",
        )
        owned[layer] = own_grads
    sum_attention, sum_attnbias, sum_combiner, sum_expander, sum_expbias, sum_reducer = [
        jnp.stack([owned[layer][index] for layer in range(layer_count)]) for index in range(6)
    ]
    spread_rows = lax.dynamic_update_slice_in_dim(
        jnp.zeros((group_rows, width), jnp.float32), grad_stream, start_row, 0
    )
    grad_positions = jnp.sum(spread_rows.reshape(clip_count, seq_len, width), axis=0)
    grad_placeholder = jnp.sum(jnp.where(masked, grad_stream, 0.0), axis=0)
    grad_lifted = jnp.where(masked, 0.0, grad_stream)
    grad_offsets = jnp.stack(
        [
            jnp.sum(jnp.where(is_patch, 0.0, grad_lifted), axis=0),
            jnp.sum(jnp.where(is_patch, grad_lifted, 0.0), axis=0),
        ]
    )
    lifted_round = grad_lifted.astype(jnp.bfloat16)
    grad_projector = jnp.einsum(
        "rp,rd->pd", widened, lifted_round, preferred_element_type=jnp.float32
    ).reshape(2, patch_len, width)
    both_halves = jnp.einsum(
        "rd,pd->rp", lifted_round, flat_projector, preferred_element_type=jnp.float32
    )
    grad_patches = jnp.where(is_patch, both_halves[:, patch_len:], both_halves[:, :patch_len])
    grad_scales = jnp.stack(gain_grads)
    grad_shifts = jnp.stack(shift_grads)
    grad_combbias = jnp.stack(comb_grads)
    grad_redbias = jnp.stack(red_grads)
    (
        grad_scales,
        grad_shifts,
        grad_combbias,
        grad_redbias,
        grad_projector,
        grad_offsets,
        grad_placeholder,
        grad_positions,
    ) = lax.psum(
        (
            grad_scales,
            grad_shifts,
            grad_combbias,
            grad_redbias,
            grad_projector,
            grad_offsets,
            grad_placeholder,
            grad_positions,
        ),
        ("wide", "narrow"),
    )
    return (
        stream,
        grad_patches,
        grad_projector,
        grad_offsets,
        grad_placeholder,
        grad_positions,
        grad_scales,
        grad_shifts,
        sum_attention,
        sum_attnbias,
        sum_combiner,
        grad_combbias,
        sum_expander,
        sum_expbias,
        sum_reducer,
        grad_redbias,
    )


def solution(mesh):
    return jax.shard_map(
        per_device,
        mesh=mesh,
        in_specs=(
            P(("wide", "narrow"), None),
            P(("wide", "narrow")),
            P("wide", None),
            P(),
            P(),
            P(),
            P(),
            P(),
            P(),
            P(None, None, None, "narrow"),
            P(None, None, "narrow"),
            P(None, "narrow", None),
            P(),
            P(None, None, "narrow"),
            P(None, "narrow"),
            P(None, "narrow", None),
            P(),
            P(("wide", "narrow"), None),
        ),
        out_specs=(
            P(("wide", "narrow"), None),
            P(("wide", "narrow"), None),
            P(),
            P(),
            P(),
            P(),
            P(),
            P(),
            P(None, None, None, "narrow"),
            P(None, None, "narrow"),
            P(None, "narrow", None),
            P(),
            P(None, None, "narrow"),
            P(None, "narrow"),
            P(None, "narrow", None),
            P(),
        ),
        check_vma=False,
    )
```

profile of v0, /device:TPU:0, one launch (start us, length us, event | category | flops | bytes accessed | tf_op | source)
XLA Modules:
  0.0 964.2 jit_solution(6585855473328736234)
XLA Ops:
  15.2 10.1 %all_gather.24 = bf16[512,768]{1,0:T(8,128)(2,1)S(1)} all-gather(bf16[128,768]{1,0:T(8,128)(2,1)S(1)} %add_convert_fusion.3), channel_id=1, replica_groups=mesh['wide'=8,'narrow'=4] {'narrow'}, dimensions={0}, use_global_device_ids=true | all-gather | bytes 983040 | tf_op jit(solution)/shard_map/all_gather | solution.py:29
  32.6 23.0 %reduce-scatter.9.cloned.1.call-done = bf16[128,768]{1,0:T(8,128)(2,1)} async-done(((bf16[512,768]{1,0:T(8,128)(2,1)}), bf16[128,768]{1,0:T(8,128)(2,1)}) %reduce-scatter.9.cloned.1.call-update) | async-done | bytes 196624 | tf_op jit(solution)/shard_map/reduce_scatter | solution.py:41
  57.1 8.2 all_gather.25
  65.4 5.4 multiply_convert_fusion.3
  74.1 23.1 %reduce-scatter.11.cloned.1.call-done = bf16[128,768]{1,0:T(8,128)(2,1)} async-done(((bf16[512,768]{1,0:T(8,128)(2,1)}), bf16[128,768]{1,0:T(8,128)(2,1)}) %reduce-scatter.11.cloned.1.call-update) | async-done | bytes 196624 | tf_op jit(solution)/shard_map/reduce_scatter | solution.py:41
  98.8 8.2 all_gather.26
  110.2 1.7 squeeze.116
  112.0 2.0 fusion.70
  122.2 10.1 %all_gather.28 = bf16[512,768]{1,0:T(8,128)(2,1)} all-gather(bf16[128,768]{1,0:T(8,128)(2,1)} %param.35), channel_id=1, replica_groups=mesh['wide'=8,'narrow'=4] {'narrow'}, dimensions={0}, use_global_device_ids=true | all-gather | bytes 983040 | tf_op jit(solution)/shard_map/all_gather | solution.py:33
  132.3 13.6 %reduce-scatter.13.cloned.1.call-done = bf16[128,768]{1,0:T(8,128)(2,1)} async-done(((bf16[512,768]{1,0:T(8,128)(2,1)}), bf16[128,768]{1,0:T(8,128)(2,1)}) %reduce-scatter.13.cloned.1.call-update) | async-done | bytes 196624 | tf_op jit(solution)/shard_map/reduce_scatter | solution.py:41
  148.1 8.4 all_gather.27
  156.5 10.9 %multiply_convert_fusion.2 = (bf16[512,768]{1,0:T(8,128)(2,1)}, f32[512,768]{1,0:T(8,128)S(1)}, f32[512,768]{1,0:T(8,128)S(1)}) fusion(f32[768]{0:T(1024)S(1)} %copy-done.119, bf16[512,768]{1,0:T(8,128)(2,1)S(1)} %all_gather.27, bf16[2,768,768]{2,1,0:T(8,128)(2,1)S(1)} %copy-done.133), kind=kOutput, calls=%fused_computation.19 | convolution fusion | flops 629932032 | bytes 5902336 | tf_op jit(solution)/shard_map/dot_general | solution.py:182
  167.5 1.8 fusion.132
  171.9 3.2 convolution_convert_fusion.2
  175.9 19.7 %reduce-scatter.17.cloned.1.call-done = bf16[128,768]{1,0:T(8,128)(2,1)} async-done(((bf16[512,768]{1,0:T(8,128)(2,1)}), bf16[128,768]{1,0:T(8,128)(2,1)}) %reduce-scatter.17.cloned.1.call-update) | async-done | bytes 196624 | tf_op jit(solution)/shard_map/reduce_scatter | solution.py:54
  195.6 1.9 fusion.64
  198.6 22.7 %reduce-scatter.15.cloned.1.call-done = bf16[128,768]{1,0:T(8,128)(2,1)} async-done(((bf16[512,768]{1,0:T(8,128)(2,1)}), bf16[128,768]{1,0:T(8,128)(2,1)}) %reduce-scatter.15.cloned.1.call-update) | async-done | bytes 196624 | tf_op jit(solution)/shard_map/reduce_scatter | solution.py:41
  221.3 2.2 fusion.122
  224.3 8.2 all_gather.29
  236.2 2.7 convert_reduce_fusion.5
  245.0 23.8 %reduce-scatter.19.cloned.1.call-done = bf16[128,768]{1,0:T(8,128)(2,1)} async-done(((bf16[512,768]{1,0:T(8,128)(2,1)}), bf16[128,768]{1,0:T(8,128)(2,1)}) %reduce-scatter.19.cloned.1.call-update) | async-done | bytes 196624 | tf_op jit(solution)/shard_map/reduce_scatter | solution.py:54
  268.8 1.8 convert_reduce_fusion.2
  271.2 1.8 fusion.65
  273.0 2.2 convert_reduce_fusion.4
  276.0 8.4 all_gather.30
  284.4 3.5 fusion.133
  290.7 3.6 convolution_bitcast_fusion.2
  294.2 20.1 %reduce-scatter.21.cloned.1.call-done = bf16[128,768]{1,0:T(8,128)(2,1)} async-done(((bf16[512,768]{1,0:T(8,128)(2,1)}), bf16[128,768]{1,0:T(8,128)(2,1)}) %reduce-scatter.21.cloned.1.call-update) | async-done | bytes 196624 | tf_op jit(solution)/shard_map/reduce_scatter | solution.py:54
  314.4 1.7 convert_reduce_fusion.1
  316.1 1.8 fusion.66
  317.9 1.9 fusion.121
  319.8 8.2 all_gather.31
  335.8 1.7 convolution_convert_fusion.4
  337.6 3.4 convolution_bitcast_fusion
  342.5 1.9 fusion.137
  344.4 2.2 convolution_bitcast_fusion.3
  346.6 2.2 convolution_bitcast_fusion.1
  350.3 1.9 fusion.136
  355.8 38.5 %all-reduce.2 = (f32[1,2,192]{2,1,0:T(2,128)S(1)}, f32[1,2,192]{2,1,0:T(2,128)S(1)}, f32[1,768]{1,0:T(1,128)S(1)}, f32[1,768]{1,0:T(1,128)S(1)}) all-reduce(f32[1,2,192]{2,1,0:T(2,128)S(1)} %maximum_bitcast_fusion.5, f32[1,2,192]{2,1,0:T(2,128)S(1)} %maximum_bitcast_fusion.4, ...), channel_id=1, replica_groups=mesh['wide'=8,'narrow'=4] {'wide'}, use_global_device_ids=true, to_apply=%region_56.57 | all-reduce | flops 2304 | bytes 18432 | tf_op jit(solution)/shard_map/psum | solution.py:305
  399.7 1.8 select_reduce_fusion.2
  405.3 43.3 %all-reduce = (f32[2,768]{1,0:T(2,128)}, f32[768]{0:T(1024)}, f32[2,2,768]{2,1,0:T(2,128)}, f32[2,2,768]{2,1,0:T(2,128)}, f32[2,768]{1,0:T(2,128)}, /*index=5*/f32[2,768]{1,0:T(2,128)}) all-reduce(f32[2,768]{1,0:T(2,128)S(1)} %pad_maximum_fusion.9, ...), channel_id=1, replica_groups=mesh['wide'=8,'narrow'=4] {'wide','narrow'}, use_global_device_ids=true, to_apply=%region_34.35 | all-reduce | flops 11520 | bytes 92160 | tf_op jit(solution)/shard_map/psum | solution.py:353
  449.7 363.3 %all-reduce.9.cloned.1.call-done = (f32[1,3,768,192]{2,3,1,0:T(8,128)}, f32[1,3,768,192]{2,3,1,0:T(8,128)}, f32[1,192,768]{2,1,0:T(8,128)}, f32[1,192,768]{2,1,0...) async-done(((f32[1,3,768,192]{2,3,1,0:T(8,128)}, f32[1,3,768,192]{2,3,1,0:T(8,128)}, ...) | async-done | bytes 14155792 | tf_op jit(solution)/shard_map/psum | solution.py:305
  813.0 2.5 pad_maximum_fusion.3
  815.5 3.7 pad_maximum_fusion.2
  819.2 2.7 pad_maximum_fusion
  823.3 2.5 pad_maximum_fusion.1
  825.8 127.5 %all-reduce.7.cloned.1.call-done = (f32[2,256,768]{2,1,0:T(8,128)}, f32[256,768]{1,0:T(8,128)}) async-done(((f32[2,256,768]{2,1,0:T(8,128)}, f32[256,768]{1,0:T(8,128)}), (f32[2,256,768]{2,1,0:T(8,128)}, f32[256,768]{1,0:T(8,128)})) %all-reduce.7.cloned.1.call-update) | async-done | bytes 2359312 | tf_op jit(solution)/shard_map/psum | solution.py:353
  953.3 2.7 copy.210
  (451 shorter events, 80.1 us)
Async XLA Ops:
  7.2 48.4 %reduce-scatter.9.cloned.1.call-start = ((), (), s32[]{:S(2)}) async-start(), calls=%async_computation.8 | async-start | bytes 983040 | tf_op jit(solution)/shard_map/reduce_scatter | solution.py:41
  13.7 11.6 %copy-start.29 = (bf16[2,3,768,192]{2,3,1,0:T(8,128)(2,1)S(1)}, bf16[2,3,768,192]{2,3,1,0:T(8,128)(2,1)}, u32[]{:S(2)}) copy-start(bf16[2,3,768,192]{2,3,1,0:T(8,128)(2,1)} %param.27) | copy-start | bytes 5308420
  14.2 12.3 %copy-start.88 = (f32[128]{0:T(128)}, f32[128]{0:T(128)S(1)}, u32[]{:S(2)}) copy-start(f32[128]{0:T(128)S(1)} %broadcast_multiply_fusion.3) | copy-start | bytes 1540
  14.4 12.0 %copy-start.111 = (f32[128]{0:T(128)}, f32[128]{0:T(128)S(1)}, u32[]{:S(2)}) copy-start(f32[128]{0:T(128)S(1)} %fusion.108) | copy-start | bytes 1540
  15.1 83.5 %copy-start.61 = (f32[768]{0:T(1024)}, f32[768]{0:T(1024)S(1)}, u32[]{:S(2)}) copy-start(f32[768]{0:T(1024)S(1)} %get-tuple-element.218) | copy-start | bytes 9220
  31.3 65.9 %reduce-scatter.11.cloned.1.call-start = ((), (), s32[]{:S(2)}) async-start(), calls=%async_computation.9 | async-start | bytes 983040 | tf_op jit(solution)/shard_map/reduce_scatter | solution.py:41
  55.6 9.8 %copy-start.132 = (bf16[2,768,768]{2,1,0:T(8,128)(2,1)S(1)}, bf16[2,768,768]{2,1,0:T(8,128)(2,1)}, u32[]{:S(2)}) copy-start(bf16[2,768,768]{2,1,0:T(8,128)(2,1)} %param.31) | copy-start | bytes 7077892
  56.8 14.0 %copy-start.90 = (f32[128]{0:T(128)}, f32[128]{0:T(128)S(1)}, u32[]{:S(2)}) copy-start(f32[128]{0:T(128)S(1)} %broadcast_multiply_fusion.2) | copy-start | bytes 1540
  57.0 13.8 %copy-start.125 = (f32[128]{0:T(128)}, f32[128]{0:T(128)S(1)}, u32[]{:S(2)}) copy-start(f32[128]{0:T(128)S(1)} %multiply_reduce_fusion.4) | copy-start | bytes 1540
  57.0 13.8 %copy-start.113 = (f32[128]{0:T(128)}, f32[128]{0:T(128)S(1)}, u32[]{:S(2)}) copy-start(f32[128]{0:T(128)S(1)} %fusion.109) | copy-start | bytes 1540
  65.4 6.3 copy-start.129
  73.4 72.5 %reduce-scatter.13.cloned.1.call-start = ((), (), s32[]{:S(2)}) async-start(), calls=%async_computation.10 | async-start | bytes 983040 | tf_op jit(solution)/shard_map/reduce_scatter | solution.py:41
  97.2 10.6 %copy-start.11 = (bf16[1,3,768,192]{2,3,1,0:T(8,128)(2,1)S(1)}, bf16[1,3,768,192]{2,3,1,0:T(8,128)(2,1)}, u32[]{:S(2)}) copy-start(bf16[1,3,768,192]{2,3,1,0:T(8,128)(2,1)} %get-tuple-element.179) | copy-start | bytes 2654212
  98.4 8.6 copy-start.92
  98.6 8.4 copy-start.127
  98.6 8.4 copy-start.115
  122.1 25.8 %copy-start.66 = (f32[768]{0:T(1024)S(1)}, f32[768]{0:T(1024)}, u32[]{:S(2)}) copy-start(f32[768]{0:T(1024)} %get-tuple-element.221) | copy-start | bytes 9220
  122.1 25.8 %copy-start.75 = (f32[768]{0:T(1024)S(1)}, f32[768]{0:T(1024)}, u32[]{:S(2)}) copy-start(f32[768]{0:T(1024)} %get-tuple-element.130) | copy-start | bytes 9220
  122.1 73.5 %reduce-scatter.17.cloned.1.call-start = ((), (), s32[]{:S(2)}) async-start(), calls=%async_computation.12 | async-start | bytes 983040 | tf_op jit(solution)/shard_map/reduce_scatter | solution.py:54
  145.9 10.5 %copy-start.119 = (f32[768]{0:T(1024)S(1)}, f32[768]{0:T(1024)}, u32[]{:S(2)}) copy-start(f32[768]{0:T(1024)} %get-tuple-element.136) | copy-start | bytes 9220
  145.9 10.5 %copy-start.133 = (bf16[2,768,768]{2,1,0:T(8,128)(2,1)S(1)}, bf16[2,768,768]{2,1,0:T(8,128)(2,1)}, u32[]{:S(2)}) copy-start(bf16[2,768,768]{2,1,0:T(8,128)(2,1)} %param.31) | copy-start | bytes 7077892
  147.2 9.3 copy-start.110
  147.4 9.1 copy-start.116
  156.5 11.0 %copy-start.50 = (bf16[512,768]{1,0:T(8,128)(2,1)}, bf16[512,768]{1,0:T(8,128)(2,1)S(1)}, u32[]{:S(2)}) copy-start(bf16[512,768]{1,0:T(8,128)(2,1)S(1)} %all_gather.27) | copy-start | bytes 2359300
  156.5 11.0 %copy-start.48 = (bf16[512,768]{1,0:T(8,128)(2,1)S(1)}, bf16[512,768]{1,0:T(8,128)(2,1)}, u32[]{:S(2)}) copy-start(bf16[512,768]{1,0:T(8,128)(2,1)} %all_gather.28) | copy-start | bytes 2359300
  156.5 11.0 %copy-start.130 = (bf16[2,768,768]{2,1,0:T(8,128)(2,1)S(1)}, bf16[2,768,768]{2,1,0:T(8,128)(2,1)}, u32[]{:S(2)}) copy-start(bf16[2,768,768]{2,1,0:T(8,128)(2,1)} %param.33) | copy-start | bytes 7077892
  171.8 49.5 %reduce-scatter.15.cloned.1.call-start = ((), (), s32[]{:S(2)}) async-start(), calls=%async_computation.11 | async-start | bytes 983040 | tf_op jit(solution)/shard_map/reduce_scatter | solution.py:41
  175.1 93.7 %reduce-scatter.19.cloned.1.call-start = ((), (), s32[]{:S(2)}) async-start(), calls=%async_computation.13 | async-start | bytes 983040 | tf_op jit(solution)/shard_map/reduce_scatter | solution.py:54
  221.3 12.2 %copy-start.55 = (bf16[2,192,768]{2,1,0:T(8,128)(2,1)S(1)}, bf16[2,192,768]{2,1,0:T(8,128)(2,1)}, u32[]{:S(2)}) copy-start(bf16[2,192,768]{2,1,0:T(8,128)(2,1)} %param.29) | copy-start | bytes 1769476
  223.5 9.1 copy-start.122
  243.3 25.5 %copy-start.62 = (f32[768]{0:T(1024)S(1)}, f32[768]{0:T(1024)}, u32[]{:S(2)}) copy-start(f32[768]{0:T(1024)} %copy-done.61) | copy-start | bytes 9220
  243.3 25.5 %copy-start.93 = (f32[128]{0:T(128)S(1)}, f32[128]{0:T(128)}, u32[]{:S(2)}) copy-start(f32[128]{0:T(128)} %copy-done.92) | copy-start | bytes 1540
  245.0 69.4 %reduce-scatter.21.cloned.1.call-start = ((), (), s32[]{:S(2)}) async-start(), calls=%async_computation.14 | async-start | bytes 983040 | tf_op jit(solution)/shard_map/reduce_scatter | solution.py:54
  268.8 15.6 %copy-start.140 = (f32[512,768]{1,0:T(8,128)S(1)}, f32[512,768]{1,0:T(8,128)}, u32[]{:S(2)}) copy-start(f32[512,768]{1,0:T(8,128)} %get-tuple-element.176) | copy-start | bytes 4718596
  273.0 11.3 %copy-start.131 = (bf16[2,768,768]{2,1,0:T(8,128)(2,1)S(1)}, bf16[2,768,768]{2,1,0:T(8,128)(2,1)}, u32[]{:S(2)}) copy-start(bf16[2,768,768]{2,1,0:T(8,128)(2,1)} %param.33) | copy-start | bytes 7077892
  290.5 105.6 %reduce-scatter.23.cloned.1.call-start = ((), (), s32[]{:S(2)}) async-start(), calls=%async_computation.15 | async-start | bytes 983040 | tf_op jit(solution)/shard_map/reduce_scatter | solution.py:54
  290.6 23.7 %copy-start.91 = (f32[128]{0:T(128)S(1)}, f32[128]{0:T(128)}, u32[]{:S(2)}) copy-start(f32[128]{0:T(128)} %copy-done.90) | copy-start | bytes 1540
  290.6 25.5 %copy-start.126 = (f32[128]{0:T(128)S(1)}, f32[128]{0:T(128)}, u32[]{:S(2)}) copy-start(f32[128]{0:T(128)} %copy-done.125) | copy-start | bytes 1540
  290.6 25.5 %copy-start.114 = (f32[128]{0:T(128)S(1)}, f32[128]{0:T(128)}, u32[]{:S(2)}) copy-start(f32[128]{0:T(128)} %copy-done.113) | copy-start | bytes 1540
  317.9 11.0 %copy-start.56 = (bf16[2,192,768]{2,1,0:T(8,128)(2,1)S(1)}, bf16[2,192,768]{2,1,0:T(8,128)(2,1)}, u32[]{:S(2)}) copy-start(bf16[2,192,768]{2,1,0:T(8,128)(2,1)} %param.29) | copy-start | bytes 1769476
  337.5 475.5 %all-reduce.9.cloned.1.call-start = ((), (), s32[]{:S(2)}) async-start(), calls=%async_computation.17 | async-start | bytes 28311552 | tf_op jit(solution)/shard_map/psum | solution.py:305
  352.3 43.8 %copy-start.89 = (f32[128]{0:T(128)S(1)}, f32[128]{0:T(128)}, u32[]{:S(2)}) copy-start(f32[128]{0:T(128)} %copy-done.88) | copy-start | bytes 1540
  352.3 45.5 %copy-start.124 = (f32[128]{0:T(128)S(1)}, f32[128]{0:T(128)}, u32[]{:S(2)}) copy-start(f32[128]{0:T(128)} %copy-done.123) | copy-start | bytes 1540
  352.4 45.5 %copy-start.112 = (f32[128]{0:T(128)S(1)}, f32[128]{0:T(128)}, u32[]{:S(2)}) copy-start(f32[128]{0:T(128)} %copy-done.111) | copy-start | bytes 1540
  352.4 47.3 %copy-start.102 = (pred[128]{0:T(512)(128)(4,1)S(1)}, pred[128]{0:T(512)(128)(4,1)}, u32[]{:S(2)}) copy-start(pred[128]{0:T(512)(128)(4,1)} %copy-done.101) | copy-start | bytes 388
  352.4 47.3 %copy-start.105 = (pred[128]{0:T(512)(128)(4,1)S(1)}, pred[128]{0:T(512)(128)(4,1)}, u32[]{:S(2)}) copy-start(pred[128]{0:T(512)(128)(4,1)} %copy-done.104) | copy-start | bytes 388
  352.4 600.9 %all-reduce.7.cloned.1.call-start = ((), (), s32[]{:S(2)}) async-start(), calls=%async_computation.16 | async-start | bytes 4718592 | tf_op jit(solution)/shard_map/psum | solution.py:353
  404.5 44.4 %copy-start.103 = (pred[128]{0:T(512)(128)(4,1)S(1)}, pred[128]{0:T(512)(128)(4,1)}, u32[]{:S(2)}) copy-start(pred[128]{0:T(512)(128)(4,1)} %copy-done.101) | copy-start | bytes 388
  (103 other events, 181.3 us)
Sparse Core Ops, SparseCore 0:
  31.4 24.1 reduce-scatter.8
  73.5 23.6 reduce-scatter.10
  122.2 23.6 reduce-scatter.12
  171.9 23.6 reduce-scatter.16
  198.0 23.2 reduce-scatter.14
  245.1 23.6 reduce-scatter.18
  290.7 23.6 reduce-scatter.20
  337.6 23.6 reduce-scatter.22
  367.4 445.5 all-reduce.8
  819.0 134.2 all-reduce.6
where the time goes:
time: 973 us; the launch traced here: 964 us
  waiting for transfers between devices  637 us (65%)
  blocking collectives  152 us (16%)
  matrix products  68.6 us (7%)
  other arithmetic  54.3 us (6%)
  local copies, waits for them, and re-layouts  36.1 us (4%)
  between operations  16.2 us (2%)
    psum x1, waiting for transfers between devices, per_device(): lax.psum((grad_attention, grad_attnbias, grad_combiner, grad_expander, gr...  363 us
    psum x1, waiting for transfers between devices, per_device(): lax.psum((grad_scales, grad_shifts, grad_combbias, grad_redbias, grad_pro...  128 us
    reduce_scatter x4, waiting for transfers between devices, sum_forward(): lax.psum_scatter(term(jnp.int32(0), local_rows * lax.axis_size('narrow'))...  82.4 us
    reduce_scatter x4, waiting for transfers between devices, sum_backward(): lax.psum_scatter(term(jnp.int32(0), local_rows * lax.axis_size('narrow'))...  63.6 us
    psum x1, blocking collectives, per_device(): lax.psum((grad_scales, grad_shifts, grad_combbias, grad_redbias, grad_pro...  43.3 us
    psum x1, blocking collectives, per_device(): lax.psum((grad_attention, grad_attnbias, grad_combiner, grad_expander, gr...  38.5 us
    all_gather x4, blocking collectives, share_grads(): return lax.all_gather(values, 'narrow', axis=0, tiled=True)  35 us
    all_gather x4, blocking collectives, share_rows(): return lax.all_gather(values, 'narrow', axis=0, tiled=True)  34.9 us
  transfers between devices with their start and end apart: 10, of which 9 were waited for; matrix products, arithmetic and copies ran while one was open for 5% of the time, Pallas kernels for 0%

commit v1 on v0

v1 whole, which is shorter than its diff:
```python
import functools

import jax
import jax.numpy as jnp
from jax import lax
from jax.experimental import pallas as pl
from jax.experimental.pallas import tpu as pltpu
from jax.sharding import PartitionSpec as P

HD = 64
EPS = 1e-06
BF = jnp.bfloat16
F32 = jnp.float32
MESH = pl.DeviceIdType.MESH


def nn(left, right):
    return jnp.dot(left, right, preferred_element_type=F32)


def nt(left, right):
    return lax.dot_general(left, right, (((1,), (1,)), ((), ())), preferred_element_type=F32)


def tn(left, right):
    return lax.dot_general(left, right, (((0,), (0,)), ((), ())), preferred_element_type=F32)


def loop(count, body):
    def step(index, carry):
        body(index)
        return carry

    lax.fori_loop(0, count, step, 0)


def hat_of(values):
    center = values - jnp.mean(values, axis=-1, keepdims=True)
    variance = jnp.mean(center * center, axis=-1, keepdims=True)
    scale = lax.rsqrt(variance + EPS)
    return center * scale, scale


def column_sums(values):
    return jnp.sum(values, axis=0, keepdims=True)


class Copy:
    def __init__(self, src, dst, send, recv, target):
        self.args = dict(src_ref=src, dst_ref=dst, send_sem=send, recv_sem=recv, device_id=target, device_id_type=MESH)

    def start(self):
        pltpu.make_async_remote_copy(**self.args).start()

    def wait(self):
        pltpu.make_async_remote_copy(**self.args).wait()

    def wait_send(self):
        pltpu.make_async_remote_copy(**self.args).wait_send()

    def wait_recv(self):
        pltpu.make_async_remote_copy(**self.args).wait_recv()


def add_into(dst, dst_row, src, src_row, rows):
    block = next(b for b in (96, 64, 112, 48, 32, 16) if rows % b == 0)

    def step(index):
        into = pl.ds(pl.multiple_of(dst_row + index * block, 16), block)
        give = pl.ds(pl.multiple_of(src_row + index * block, 16), block)
        dst[into, :] = (dst[into, :].astype(F32) + src[give, :].astype(F32)).astype(BF)

    loop(rows // block, step)


class Place:
    def __init__(self, wide_count):
        self.w = lax.axis_index("wide")
        self.n = lax.axis_index("narrow")
        self.y = self.n // 2
        self.c = self.n % 2
        self.x = self.w % 2
        self.z = self.w // 2
        line = wide_count // 2
        self.half = line // 2
        self.low = self.z < self.half
        self.side = jnp.where(self.low, 0, 1)
        self.depth = jnp.where(self.low, self.z, line - 1 - self.z)
        step = jnp.where(self.low, 2, -2)
        self.sibling = (self.w, self.n + 1 - 2 * self.c)
        self.partner = (self.w, self.n + 2 - 4 * self.y)
        self.pair = (self.w + 1 - 2 * self.x, self.n)
        self.inward = (self.w + step, self.n)
        self.outward = (self.w - jnp.where(self.depth > 0, step, -step), self.n)
        self.has_out = self.depth > 0
        self.inner = self.depth == self.half - 1


def hops(count, hop):
    if count == 1:
        hop(0)
    elif count > 1:
        loop(count, hop)


class PairFirst:
    def __init__(self, place, total, row, rows, buf, at, out, send, recv, store):
        self.place, self.total, self.buf = place, total, buf
        half = rows // 2
        self.half, self.at = half, at
        mine = pl.multiple_of(row + place.x * half, 16)
        other = pl.multiple_of(row + (1 - place.x) * half, 16)
        self.mine = mine
        keep, give = total.at[pl.ds(mine, half)], total.at[pl.ds(other, half)]
        out_keep, out_give = out.at[pl.ds(mine, half)], out.at[pl.ds(other, half)]
        slots = [buf.at[pl.ds(at + k * half, half)] for k in range(3)]
        self.pair_in = Copy(give, slots[0], send.at[0], recv.at[0], place.pair)
        self.line_in = Copy(keep, slots[1], send.at[1], recv.at[1], place.inward)
        self.middle = Copy(keep, slots[2], send.at[2], recv.at[2], place.inward)
        self.line_out = Copy(keep, out_keep, send.at[3], recv.at[3], place.outward)
        self.line_on = Copy(out_keep, out_keep, send.at[3], recv.at[3], place.outward)
        self.pair_out = Copy(keep, out_keep, send.at[4], recv.at[4], place.pair)
        self.pair_on = Copy(out_keep, out_keep, send.at[4], recv.at[4], place.pair)
        self.other = Copy(out_give, out_give, send.at[4], recv.at[4], place.pair)
        self.store = pltpu.make_async_copy(keep, out_keep, store)
        self.stages = [self.s0, self.s1, self.s2, self.s3, self.s4, self.s5]

    def s0(self):
        self.pair_in.start()

    def s1(self):
        place = self.place
        self.pair_in.wait()
        add_into(self.total, self.mine, self.buf, self.at, self.half)
        if place.half == 1:
            self.middle.start()
            return

        @pl.when(place.depth == 0)
        def _():
            self.line_in.start()

    def s2(self):
        place = self.place

        def hop(k):
            @pl.when(place.depth == k + 1)
            def _():
                self.line_in.wait_recv()
                add_into(self.total, self.mine, self.buf, self.at + self.half, self.half)

            @pl.when((place.depth == k + 1) & jnp.logical_not(place.inner))
            def _():
                self.line_in.start()

        hops(place.half - 1, hop)
        if place.half > 1:

            @pl.when(place.inner)
            def _():
                self.middle.start()

    def s3(self):
        place = self.place

        @pl.when(place.inner)
        def _():
            self.middle.wait()
            add_into(self.total, self.mine, self.buf, self.at + 2 * self.half, self.half)
            if place.half > 1:
                self.line_out.start()
            self.pair_out.start()
            self.store.start()

    def s4(self):
        place = self.place

        def hop(k):
            @pl.when(place.depth == place.half - 2 - k)
            def _():
                self.line_on.wait_recv()
                self.pair_on.start()

            @pl.when((place.depth == place.half - 2 - k) & place.has_out)
            def _():
                self.line_on.start()

        hops(place.half - 1, hop)

    def s5(self):
        place = self.place

        @pl.when(place.inner)
        def _():
            self.store.wait()

        if place.half > 1:

            @pl.when(jnp.logical_not(place.inner))
            def _():
                self.line_in.wait_send()

            @pl.when(place.has_out)
            def _():
                self.line_out.wait_send()

        self.pair_out.wait_send()
        self.other.wait_recv()


class LineFirst:
    def __init__(self, place, total, row, rows, buf, at, out, send, recv, store):
        self.place, self.total, self.buf = place, total, buf
        half = rows // 2
        self.row, self.rows, self.half, self.at = row, rows, half, at
        mine = pl.multiple_of(row + place.side * half, 16)
        other = pl.multiple_of(row + (1 - place.side) * half, 16)
        self.mine = mine
        whole = total.at[pl.ds(row, rows)]
        keep, give = total.at[pl.ds(mine, half)], total.at[pl.ds(other, half)]
        out_keep, out_give = out.at[pl.ds(mine, half)], out.at[pl.ds(other, half)]
        self.line_in = Copy(whole, buf.at[pl.ds(at, rows)], send.at[0], recv.at[0], place.inward)
        self.middle = Copy(give, buf.at[pl.ds(at + rows, half)], send.at[1], recv.at[1], place.inward)
        self.across = Copy(keep, buf.at[pl.ds(at + rows + half, half)], send.at[2], recv.at[2], place.pair)
        self.middle_out = Copy(keep, out_keep, send.at[3], recv.at[3], place.inward)
        self.middle_back = Copy(out_give, out_give, send.at[3], recv.at[3], place.inward)
        self.keep_out = Copy(keep, out_keep, send.at[4], recv.at[4], place.outward)
        self.keep_on = Copy(out_keep, out_keep, send.at[4], recv.at[4], place.outward)
        self.give_on = Copy(out_give, out_give, send.at[5], recv.at[5], place.outward)
        self.store = pltpu.make_async_copy(keep, out_keep, store)
        self.stages = [self.s0, self.s1, self.s2, self.s3, self.s4, self.s5]

    def s0(self):
        place = self.place
        if place.half == 1:
            self.middle.start()
            return

        @pl.when(place.depth == 0)
        def _():
            self.line_in.start()

    def s1(self):
        place = self.place

        def hop(k):
            @pl.when(place.depth == k + 1)
            def _():
                self.line_in.wait_recv()
                add_into(self.total, self.row, self.buf, self.at, self.rows)

            @pl.when((place.depth == k + 1) & jnp.logical_not(place.inner))
            def _():
                self.line_in.start()

        hops(place.half - 1, hop)
        if place.half > 1:

            @pl.when(place.inner)
            def _():
                self.middle.start()

    def s2(self):
        @pl.when(self.place.inner)
        def _():
            self.middle.wait()
            add_into(self.total, self.mine, self.buf, self.at + self.rows, self.half)
            self.across.start()

    def s3(self):
        place = self.place

        @pl.when(place.inner)
        def _():
            self.across.wait()
            add_into(self.total, self.mine, self.buf, self.at + self.rows + self.half, self.half)
            self.middle_out.start()
            if place.half > 1:
                self.keep_out.start()
            self.store.start()

    def s4(self):
        place = self.place

        @pl.when(place.inner)
        def _():
            self.middle_back.wait_recv()
            if place.half > 1:
                self.give_on.start()

    def s5(self):
        place = self.place

        def hop(k):
            @pl.when(place.depth == place.half - 2 - k)
            def _():
                self.keep_on.wait_recv()
                self.give_on.wait_recv()

            @pl.when((place.depth == place.half - 2 - k) & place.has_out)
            def _():
                self.keep_on.start()
                self.give_on.start()

        hops(place.half - 1, hop)

        @pl.when(place.inner)
        def _():
            self.middle_out.wait_send()
            self.store.wait()

        if place.half > 1:

            @pl.when(jnp.logical_not(place.inner))
            def _():
                self.line_in.wait_send()

            @pl.when(place.has_out)
            def _():
                self.keep_out.wait_send()
                self.give_on.wait_send()


def encoder(
    wide_count,
    rows_in,
    cot_in,
    slots_in,
    proj_in,
    offs_in,
    plc_in,
    pos_in,
    scales,
    shifts,
    att_in,
    abias_in,
    comb_in,
    cbias,
    exp_in,
    ebias_in,
    red_in,
    rbias,
    sums_out,
    shared_out,
    encoded_out,
    patches_out,
    wa,
    wc,
    we,
    wr,
    abias,
    ebias,
    proj,
    pos,
    rows_all,
    grad,
    stream,
    middle,
    first,
    second,
    qkv,
    probs,
    mixed,
    slope,
    hidden,
    out_round,
    pre,
    mid_round,
    grad_mixed,
    grad_qkv,
    key_acc,
    acc,
    give,
    take,
    take_top,
    cot,
    send_part,
    recv_part,
    total,
    ring,
    shared,
    shared_buf,
    top_own,
    top_other,
    patch_own,
    patch_other,
    small,
    bias_rows,
    load_sem,
    weight_send,
    weight_recv,
    rows_send,
    rows_recv,
    y_send,
    y_recv,
    part_send,
    part_recv,
    ring_send,
    ring_recv,
    shared_send,
    shared_recv,
    last_send,
    last_recv,
    store_sem,
    credit,
):
    place = Place(wide_count)
    y, c, w, n = place.y, place.c, place.w, place.n
    sibling, partner = place.sibling, place.partner
    local, width = cot_in.shape
    patch = proj_in.shape[0] // 2
    seq = pos_in.shape[0]
    layers = scales.shape[0]
    cols = att_in.shape[3]
    heads = cols // HD
    hid = exp_in.shape[2]
    scale = HD ** (-0.5)
    diagonal = y == c
    chunks = seq // local

    barrier = pltpu.get_barrier_semaphore()
    for step in (1, 2, 3):
        pl.semaphore_signal(barrier, 1, device_id=(w, (n + step) % 4), device_id_type=MESH)
    pl.semaphore_signal(barrier, 1, device_id=place.pair, device_id_type=MESH)
    pl.semaphore_signal(barrier, 1, device_id=place.inward, device_id_type=MESH)

    @pl.when(place.has_out)
    def _():
        pl.semaphore_signal(barrier, 1, device_id=place.outward, device_id_type=MESH)
        pl.semaphore_wait(barrier, 6)

    @pl.when(jnp.logical_not(place.has_out))
    def _():
        pl.semaphore_wait(barrier, 5)

    def span(index, size):
        return pl.ds(pl.multiple_of(index * size, size), size)

    far = (w, 2 - y)
    near = (w, 3 * y)
    here = span(c, local)
    row_copies = []
    for k, (src, dst) in enumerate(((rows_in, rows_all), (cot_in, cot))):
        row_copies.append(
            (
                Copy(src, dst.at[here], rows_send.at[k, 0], rows_recv.at[k, c], far),
                Copy(src, dst.at[here], rows_send.at[k, 1], rows_recv.at[k, c], near),
                pltpu.make_async_copy(src, dst.at[here], rows_recv.at[k, c]),
            )
        )

    def send_rows(k):
        to_far, to_near, to_self = row_copies[k]
        to_far.start()

        @pl.when(diagonal)
        def _():
            to_self.start()

        @pl.when(jnp.logical_not(diagonal))
        def _():
            to_near.start()

    def wait_rows(k, dst):
        for h in range(2):
            spot = dst.at[pl.ds(h * local, local)]
            pltpu.make_async_copy(spot, spot, rows_recv.at[k, h]).wait()

    send_rows(0)
    weights = []
    for layer in range(layers):
        for src, dst in ((att_in, wa), (comb_in, wc), (exp_in, we), (red_in, wr)):
            weights.append((src.at[layer], dst.at[layer]))
    own_loads = [pltpu.make_async_copy(src, dst.at[0], load_sem.at[k]) for k, (src, dst) in enumerate(weights)]
    sib_loads = [
        Copy(src, dst.at[1], weight_send.at[k], weight_recv.at[k], sibling) for k, (src, dst) in enumerate(weights)
    ]
    proj_load = pltpu.make_async_copy(proj_in, proj, load_sem.at[8])
    pos_load = pltpu.make_async_copy(pos_in, pos, load_sem.at[9])
    abias_copy = Copy(abias_in, abias.at[1], weight_send.at[8], weight_recv.at[8], sibling)
    ebias_copy = Copy(ebias_in, ebias.at[1], weight_send.at[9], weight_recv.at[9], sibling)
    abias_copy.start()
    ebias_copy.start()
    proj_load.start()
    pos_load.start()
    for k in range(8):
        own_loads[k].start()
        sib_loads[k].start()
        if k == 3:
            send_rows(1)
    abias[0] = abias_in[...]
    ebias[0] = ebias_in[...]
    small[...] = jnp.zeros_like(small)
    bias_rows[...] = jnp.zeros_like(bias_rows)

    def need(k):
        own_loads[k].wait()
        sib_loads[k].wait_recv()

    def note(row, values):
        small[row : row + 1, :] += column_sums(values)

    def param(ref, layer, row):
        return ref[layer, row : row + 1, :].astype(F32)

    def y_copy(index, slot, rows):
        return Copy(
            give.at[slot, rows], take.at[slot, rows], y_send.at[index[0], index[1]], y_recv.at[index[0], index[1]], partner
        )

    def offer(exchange, slot, ch, values):
        rows = span(ch, local)
        give[slot, rows, :] = values.astype(BF)
        y_copy((exchange, ch), slot, rows).start()

    def collect(exchange, slot, ch):
        rows = span(ch, local)
        y_copy((exchange, ch), slot, rows).wait()
        return give[slot, rows, :].astype(F32) + take[slot, rows, :].astype(F32)

    def head_mask(rows, h):
        lane = lax.broadcasted_iota(jnp.int32, (rows, cols), 1)
        return (lane >= h * HD) & (lane < (h + 1) * HD)

    place_col = lax.broadcasted_iota(jnp.int32, (seq, slots_in.shape[1]), 0)
    slot_row = slots_in[pl.ds(c, 1), :]
    masked = jnp.max(jnp.where(place_col == slot_row, 1.0, 0.0).astype(F32), axis=1, keepdims=True)
    wait_rows(0, rows_all)
    proj_load.wait()
    pos_load.wait()
    flags = rows_all[:, patch : patch + 128]
    wide_flags = jnp.concatenate([flags] * (patch // 128), axis=1)
    patches = rows_all[:, :patch]
    kind_one = patches * wide_flags
    kind_zero = patches - kind_one
    is_one = flags[:, 0:1].astype(F32)
    lifted = nn(kind_zero, proj[0:patch, :]) + nn(kind_one, proj[patch : 2 * patch, :])
    offset = jnp.where(is_one > 0.5, offs_in[1:2, :].astype(F32), offs_in[0:1, :].astype(F32))
    stream[0] = jnp.where(masked > 0.5, plc_in[...].astype(F32), lifted + offset) + pos[...].astype(F32)

    def before_attention(layer):
        def norm(ch):
            rows = span(ch, local)
            hat, _ = hat_of(stream[layer, rows, :])
            first[layer, rows, :] = (hat * param(scales, layer, 0) + param(shifts, layer, 0)).astype(BF)

        loop(chunks, norm)

    def project(layer):
        need(4 * layer)
        if layer == 0:
            abias_copy.wait_recv()
            ebias_copy.wait_recv()

        def group(g):
            rows = first[layer]
            query = (nn(rows, wa[layer, g, 0]) + abias[g, layer, 0:1, :].astype(F32)) * scale
            qkv[layer, g, 0] = query.astype(BF)
            qkv[layer, g, 1] = nn(rows, wa[layer, g, 1]).astype(BF)
            qkv[layer, g, 2] = (nn(rows, wa[layer, g, 2]) + abias[g, layer, 1:2, :].astype(F32)).astype(BF)

        loop(2, group)

    def attend(layer, exchange, slot):
        need(4 * layer + 1)

        def chunk(ch):
            rows = span(ch, local)

            def group(g):
                total_mixed = jnp.zeros((local, cols), F32)
                query, key, value = qkv[layer, g, 0, rows, :], qkv[layer, g, 1], qkv[layer, g, 2]
                for h in range(heads):
                    scores = nt(jnp.where(head_mask(local, h), query, 0), key)
                    raised = jnp.exp(scores - jnp.max(scores, axis=-1, keepdims=True))
                    prob = (raised / jnp.sum(raised, axis=-1, keepdims=True)).astype(BF)
                    probs[layer, g * heads + h, rows, :] = prob
                    total_mixed += nn(prob, jnp.where(head_mask(seq, h), value, 0))
                mixed[layer, g, rows, :] = total_mixed.astype(BF)

            loop(2, group)
            offer(exchange, slot, ch, nn(mixed[layer, 0, rows, :], wc[layer, 0]) + nn(mixed[layer, 1, rows, :], wc[layer, 1]))

        loop(chunks, chunk)

    def to_middle(layer, exchange, slot, ch):
        rows = span(ch, local)
        values = stream[layer, rows, :] + collect(exchange, slot, ch) + cbias[layer : layer + 1, :].astype(F32)
        middle[layer, rows, :] = values
        hat, _ = hat_of(values)
        second[layer, rows, :] = (hat * param(scales, layer, 1) + param(shifts, layer, 1)).astype(BF)

    def activate(layer, g, rows):
        value = nn(second[layer, rows, :], we[layer, g]) + ebias[g, layer : layer + 1, :].astype(F32)
        cdf = 0.5 * (1.0 + lax.erf(value * (0.5**0.5)))
        hidden[layer, g, rows, :] = (value * cdf).astype(BF)
        density = jnp.exp(-0.5 * value * value) * 0.3989422804014327
        slope[layer, g, rows, :] = (cdf + value * density).astype(BF)

    def feed_back(layer, g, rows):
        grad_hidden = nt(out_round[rows, :], wr[layer, g])
        grad_pre = grad_hidden * slope[layer, g, rows, :].astype(F32)
        bias_rows[layer, g, 0:1, :] += column_sums(grad_pre)
        pre[g, rows, :] = grad_pre.astype(BF)

    def settle(row, layer, part, base, values, gain_row):
        hat, inverse = hat_of(base)
        note(2 * layer + part, values * hat)
        note(4 + 2 * layer + part, values)
        scaled = values * param(scales, layer, part)
        inner = scaled - jnp.mean(scaled, axis=-1, keepdims=True)
        return inverse * (inner - hat * jnp.mean(scaled * hat, axis=-1, keepdims=True))

    for layer in range(layers):
        before_attention(layer)
        project(layer)
        attend(layer, 2 * layer, 0)
        need(4 * layer + 2)
        need(4 * layer + 3)
        if layer + 1 < layers:

            def chunk(ch):
                rows = span(ch, local)
                to_middle(layer, 2 * layer, 0, ch)

                def group(g):
                    activate(layer, g, rows)
                    part = nn(hidden[layer, g, rows, :], wr[layer, g])

                    @pl.when(g == 0)
                    def _():
                        acc[...] = part

                    @pl.when(g == 1)
                    def _():
                        acc[...] += part

                loop(2, group)
                offer(2 * layer + 1, 1, ch, acc[...])

            loop(chunks, chunk)

            def after(ch):
                rows = span(ch, local)
                stream[layer + 1, rows, :] = (
                    middle[layer, rows, :] + collect(2 * layer + 1, 1, ch) + rbias[layer : layer + 1, :].astype(F32)
                )

            loop(chunks, after)

    pieces = []
    base = 0
    at = 0
    plan = (
        (PairFirst, 0, hid // 2),
        (PairFirst, hid // 2, hid // 2),
        (LineFirst, hid, hid // 2),
        (LineFirst, hid + hid // 2, hid // 2),
        (PairFirst, 2 * hid, 2 * cols),
        (PairFirst, 2 * hid + 2 * cols, cols),
        (LineFirst, 2 * hid + 3 * cols, cols + 32),
    )
    per_layer = len(plan)
    for layer in reversed(range(layers)):
        for kind, row, count in plan:
            k = len(pieces)
            pieces.append((kind(place, total.at[layer], row, count, ring, at, sums_out.at[layer], ring_send.at[k], ring_recv.at[k], store_sem.at[k]), layer, row, count))
            at += count // 2 * 3 if kind is PairFirst else count * 2

    def parts(k, own, other):
        piece, layer, row, count = pieces[k]
        slot = k % 2
        copy = Copy(
            send_part.at[slot, pl.ds(0, count)], recv_part.at[pl.ds(row, count)], part_send.at[k], part_recv.at[k], sibling
        )
        if k >= 2:
            old = pieces[k - 2]
            Copy(
                send_part.at[slot, pl.ds(0, old[3])],
                recv_part.at[pl.ds(old[2], old[3])],
                part_send.at[k - 2],
                part_recv.at[k - 2],
                sibling,
            ).wait_send()
        if k == per_layer:
            pl.semaphore_wait(credit, 1)
        other(send_part.at[slot])
        copy.start()
        own(total.at[layer, pl.ds(row, count)])
        copy.wait_recv()
        add_into(total.at[layer], row, recv_part, row, count)
        if k == per_layer - 1:
            pl.semaphore_signal(credit, 1, device_id=sibling, device_id_type=MESH)
        piece.stages[0]()

    done = {}

    def advance(k):
        stage = done.get(k, 1)
        if stage < 6:
            pieces[k][0].stages[stage]()
        done[k] = stage + 1

    def weight_grad(left, right, g):
        count = left.shape[1] // 128

        def into(ref):
            def step(t):
                ref[span(t, 128), :] = tn(left[:, span(t, 128)], right).astype(BF)

            loop(count, step)

        return into

    def feed_grads(layer, base):
        for t in range(2):
            cut = pl.ds(t * (hid // 2), hid // 2)
            parts(
                base + t,
                weight_grad(second.at[layer, :, cut], pre[0], 0),
                weight_grad(second.at[layer, :, cut], pre[1], 1),
            )
        for t in range(2):
            cut = pl.ds(t * (hid // 2), hid // 2)
            parts(
                base + 2 + t,
                weight_grad(hidden.at[layer, 0, :, cut], out_round[...], 0),
                weight_grad(hidden.at[layer, 1, :, cut], out_round[...], 1),
            )

    def attention_grads(layer, base):
        def stack(g, which):
            def into(ref):
                for j, index in enumerate(which):
                    ref[pl.ds(j * cols, cols), :] = tn(grad_qkv[g, index], first[layer]).astype(BF)

            return into

        def comb(g):
            def into(ref):
                ref[pl.ds(0, cols), :] = tn(mixed[layer, g], mid_round[...]).astype(BF)
                ref[pl.ds(cols, 32), :] = bias_rows[layer, g].astype(BF)

            return into

        parts(base + 4, stack(0, (0, 1)), stack(1, (0, 1)))
        parts(base + 5, stack(0, (2,)), stack(1, (2,)))
        parts(base + 6, comb(0), comb(1))

    wait_rows(1, cot)
    last = layers - 1

    def start_back(ch):
        rows = span(ch, local)
        grad[rows, :] = cot[rows, :].astype(F32)

    loop(chunks, start_back)

    def top_send():
        return Copy(top_other, top_own, last_send.at[0], last_recv.at[0], sibling)

    top_copy = Copy(give.at[2], take_top, last_send.at[1], last_recv.at[1], partner)

    for layer in reversed(range(layers)):
        base = (last - layer) * per_layer
        exchange = 4 + 2 * (last - layer)

        def chunk(ch):
            rows = span(ch, local)
            note(10 + layer, grad[rows, :])
            out_round[rows, :] = grad[rows, :].astype(BF)
            if layer == last:
                to_middle(layer, 2 * layer, 0, ch)

            def group(g):
                if layer == last:
                    activate(layer, g, rows)
                feed_back(layer, g, rows)
                part = nt(pre[g, rows, :], we[layer, g])

                @pl.when(g == 0)
                def _():
                    acc[...] = part

                @pl.when(g == 1)
                def _():
                    acc[...] += part

            loop(2, group)
            offer(exchange, 1, ch, acc[...])

        loop(chunks, chunk)

        if layer == last:

            def top(ch):
                rows = span(ch, local)
                give[2, rows, :] = (
                    nn(hidden[layer, 0, rows, :], wr[layer, 0]) + nn(hidden[layer, 1, rows, :], wr[layer, 1])
                ).astype(BF)

            loop(chunks, top)

            @pl.when(jnp.logical_not(diagonal))
            def _():
                top_copy.start()

        feed_grads(layer, base)

        def chunk(ch):
            rows = span(ch, local)
            grad_second = collect(exchange, 1, ch)
            grad_middle = grad[rows, :] + settle(rows, layer, 1, middle[layer, rows, :], grad_second, None)
            note(8 + layer, grad_middle)
            grad[rows, :] = grad_middle
            mid_round[rows, :] = grad_middle.astype(BF)

            def group(g):
                mixed_back = nt(mid_round[rows, :], wc[layer, g]).astype(BF)
                query, key, value = qkv[layer, g, 0, rows, :], qkv[layer, g, 1], qkv[layer, g, 2]
                query_acc = jnp.zeros((local, cols), F32)
                key_sum = jnp.zeros((seq, cols), F32)
                value_sum = jnp.zeros((seq, cols), F32)
                for h in range(heads):
                    prob = probs[layer, g * heads + h, rows, :]
                    back = jnp.where(head_mask(local, h), mixed_back, 0)
                    grad_probs = nt(back, value)
                    value_sum += tn(prob, back)
                    weight = prob.astype(F32)
                    center = jnp.sum(weight * grad_probs, axis=-1, keepdims=True)
                    grad_scores = (weight * (grad_probs - center)).astype(BF)
                    query_acc += nn(grad_scores, jnp.where(head_mask(seq, h), key, 0))
                    key_sum += tn(grad_scores, jnp.where(head_mask(local, h), query, 0))
                grad_query = (query_acc.astype(BF).astype(F32) * scale).astype(BF)
                grad_qkv[g, 0, rows, :] = grad_query
                bias_rows[layer, g, 1:2, 0:cols] += column_sums(grad_query.astype(F32))

                @pl.when(ch == 0)
                def _():
                    key_acc[g, 0] = key_sum
                    key_acc[g, 1] = value_sum

                @pl.when(ch > 0)
                def _():
                    key_acc[g, 0] += key_sum
                    key_acc[g, 1] += value_sum

            loop(2, group)

        loop(chunks, chunk)

        def close(g):
            grad_qkv[g, 1] = key_acc[g, 0].astype(BF)
            grad_value = key_acc[g, 1].astype(BF)
            grad_qkv[g, 2] = grad_value
            bias_rows[layer, g, 2:3, 0:cols] += column_sums(grad_value.astype(F32))

        loop(2, close)

        def chunk(ch):
            rows = span(ch, local)

            def group(g):
                part = (
                    nt(grad_qkv[g, 0, rows, :], wa[layer, g, 0])
                    + nt(grad_qkv[g, 1, rows, :], wa[layer, g, 1])
                    + nt(grad_qkv[g, 2, rows, :], wa[layer, g, 2])
                )

                @pl.when(g == 0)
                def _():
                    acc[...] = part

                @pl.when(g == 1)
                def _():
                    acc[...] += part

            loop(2, group)
            offer(exchange + 1, 0, ch, acc[...])

        loop(chunks, chunk)
        attention_grads(layer, base)

        if layer == last:

            @pl.when(jnp.logical_not(diagonal))
            def _():
                top_copy.wait_send()

            @pl.when(diagonal)
            def _():
                top_copy.wait_recv()

                def finish_top(dst, half):
                    rows = span(half, local)
                    dst[...] = (
                        middle[layer, rows, :]
                        + (give[2, rows, :].astype(F32) + take_top[rows, :].astype(F32))
                        + rbias[layer : layer + 1, :].astype(F32)
                    )

                finish_top(top_other, 1 - c)
                top_send().start()
                finish_top(top_own, c)

        def chunk(ch):
            rows = span(ch, local)
            grad_first = collect(exchange + 1, 0, ch)
            grad[rows, :] += settle(rows, layer, 0, stream[layer, rows, :], grad_first, None)

        loop(chunks, chunk)

    lifted_grad = jnp.where(masked > 0.5, 0.0, grad[...])
    note(14, grad[...] - lifted_grad)
    one_grad = jnp.where(is_one > 0.5, lifted_grad, 0.0)
    note(12, lifted_grad - one_grad)
    note(13, one_grad)
    lifted_round = lifted_grad.astype(BF)
    shared_rows = shared.shape[0]
    half_rows = shared_rows // 2
    flag_side = jnp.where(y == 1, wide_flags.astype(F32), 1.0 - wide_flags.astype(F32)).astype(BF)
    shared[0:patch, :] = tn(rows_all[:, :patch] * flag_side, lifted_round).astype(BF)
    shared[patch : patch + local, :] = grad[span(y, local), :].astype(BF)
    shared[patch + local : shared_rows, :] = small[...].astype(BF)
    keep_row, give_row = span(c, half_rows), span(1 - c, half_rows)
    shared_part = Copy(
        shared.at[give_row], shared_buf.at[pl.ds(0, half_rows)], last_send.at[2], last_recv.at[2], sibling
    )
    shared_part.start()

    patch_copy = Copy(patch_other, patch_own, last_send.at[3], last_recv.at[3], sibling)

    @pl.when(diagonal)
    def _():
        def half_back(dst, half):
            rows = span(half, local)
            flag = rows_all[rows, patch : patch + 128].astype(F32)[:, 0:1]
            masks = jnp.max(
                jnp.where(
                    lax.broadcasted_iota(jnp.int32, (local, slots_in.shape[1]), 0) + half * local == slot_row, 1.0, 0.0
                ).astype(F32),
                axis=1,
                keepdims=True,
            )
            values = jnp.where(masks > 0.5, 0.0, grad[rows, :]).astype(BF)
            dst[...] = jnp.where(flag > 0.5, nt(values, proj[patch : 2 * patch, :]), nt(values, proj[0:patch, :]))

        half_back(patch_other, 1 - c)
        patch_copy.start()
        half_back(patch_own, c)

    shared_part.wait()
    add_into(shared, pl.multiple_of(c * half_rows, 16), shared_buf, 0, half_rows)
    shared_piece = PairFirst(
        place,
        shared,
        pl.multiple_of(c * half_rows, 16),
        half_rows,
        shared_buf,
        half_rows,
        shared_out.at[y],
        shared_send,
        shared_recv,
        store_sem.at[len(pieces)],
    )
    shared_piece.stages[0]()

    count = len(pieces)
    for stage in range(1, 5):
        shared_piece.stages[stage]()
        for k in range(count):
            advance(k)
    shared_piece.stages[5]()
    across = Copy(shared_out.at[y, keep_row], shared_out.at[y, keep_row], last_send.at[4], last_recv.at[4], partner)
    across_back = Copy(
        shared_out.at[1 - y, keep_row], shared_out.at[1 - y, keep_row], last_send.at[4], last_recv.at[4], partner
    )
    across.start()
    for k in range(count):
        advance(k)
    across.wait_send()
    across_back.wait_recv()
    ends = []
    for k in range(2):
        ends.append(
            (
                Copy(
                    shared_out.at[k, keep_row], shared_out.at[k, keep_row], last_send.at[5 + k], last_recv.at[5 + k], sibling
                ),
                Copy(
                    shared_out.at[k, give_row], shared_out.at[k, give_row], last_send.at[5 + k], last_recv.at[5 + k], sibling
                ),
            )
        )
    for out, _ in ends:
        out.start()
    for out, back in ends:
        out.wait_send()
        back.wait_recv()

    @pl.when(diagonal)
    def _():
        top_send().wait_send()
        patch_copy.wait_send()

    @pl.when(jnp.logical_not(diagonal))
    def _():
        top_send().wait_recv()
        patch_copy.wait_recv()

    finals = (
        pltpu.make_async_copy(top_own, encoded_out, store_sem.at[count + 1]),
        pltpu.make_async_copy(patch_own, patches_out, store_sem.at[count + 2]),
    )
    for copy in finals:
        copy.start()
    for copy in finals:
        copy.wait()

    for to_far, to_near, _ in row_copies:
        to_far.wait_send()

        @pl.when(jnp.logical_not(diagonal))
        def _():
            to_near.wait_send()

    for copy in sib_loads + [abias_copy, ebias_copy]:
        copy.wait_send()
    for k in (count - 2, count - 1):
        piece, layer, row, size = pieces[k]
        Copy(
            send_part.at[k % 2, pl.ds(0, size)],
            recv_part.at[pl.ds(row, size)],
            part_send.at[k],
            part_recv.at[k],
            sibling,
        ).wait_send()


def per_device(
    wide_count,
    patches,
    token_kind,
    mask_slots,
    projector,
    offsets,
    placeholder,
    positions,
    scales,
    shifts,
    attention,
    attn_bias,
    combiner,
    comb_bias,
    expander,
    expand_bias,
    reducer,
    reduce_bias,
    cotangent,
):
    local, patch = patches.shape
    seq, width = positions.shape
    layers = scales.shape[0]
    cols = attention.shape[3]
    heads = cols // HD
    hid = expander.shape[2]
    flags = jnp.broadcast_to((token_kind == 1)[:, None], (local, 128)).astype(BF)
    rows_in = jnp.concatenate([patches, flags], axis=1)
    per_layer = 2 * hid + 4 * cols + 32
    shared_rows = patch + local + 64
    pieces = 7 * layers
    ring_rows = layers * (
        3 * (hid // 2) + 3 * cols + 3 * (cols // 2) + 2 * hid + 2 * (cols + 32)
    )
    vmem = pl.BlockSpec(memory_space=pltpu.VMEM)
    anyw = pl.BlockSpec(memory_space=pl.ANY)
    dma = pltpu.SemaphoreType.DMA
    scratch = [
        pltpu.VMEM((layers, 2, 3, width, cols), BF),
        pltpu.VMEM((layers, 2, cols, width), BF),
        pltpu.VMEM((layers, 2, width, hid), BF),
        pltpu.VMEM((layers, 2, hid, width), BF),
        pltpu.VMEM((2, layers, 2, cols), BF),
        pltpu.VMEM((2, layers, hid), BF),
        pltpu.VMEM((2 * patch, width), BF),
        pltpu.VMEM((seq, width), BF),
        pltpu.VMEM((seq, patch + 128), BF),
        pltpu.VMEM((seq, width), F32),
        pltpu.VMEM((layers, seq, width), F32),
        pltpu.VMEM((layers, seq, width), F32),
        pltpu.VMEM((layers, seq, width), BF),
        pltpu.VMEM((layers, seq, width), BF),
        pltpu.VMEM((layers, 2, 3, seq, cols), BF),
        pltpu.VMEM((layers, 2 * heads, seq, seq), BF),
        pltpu.VMEM((layers, 2, seq, cols), BF),
        pltpu.VMEM((layers, 2, seq, hid), BF),
        pltpu.VMEM((layers, 2, seq, hid), BF),
        pltpu.VMEM((seq, width), BF),
        pltpu.VMEM((2, seq, hid), BF),
        pltpu.VMEM((seq, width), BF),
        pltpu.VMEM((8, 128), BF),
        pltpu.VMEM((2, 3, seq, cols), BF),
        pltpu.VMEM((2, 2, seq, cols), F32),
        pltpu.VMEM((local, width), F32),
        pltpu.VMEM((3, seq, width), BF),
        pltpu.VMEM((2, seq, width), BF),
        pltpu.VMEM((seq, width), BF),
        pltpu.VMEM((seq, width), BF),
        pltpu.VMEM((2, 2 * cols, width), BF),
        pltpu.VMEM((per_layer, width), BF),
        pltpu.VMEM((layers, per_layer, width), BF),
        pltpu.VMEM((ring_rows, width), BF),
        pltpu.VMEM((shared_rows, width), BF),
        pltpu.VMEM((shared_rows // 2 + 3 * (shared_rows // 4), width), BF),
        pltpu.VMEM((local, width), F32),
        pltpu.VMEM((local, width), F32),
        pltpu.VMEM((local, patch), F32),
        pltpu.VMEM((local, patch), F32),
        pltpu.VMEM((64, width), F32),
        pltpu.VMEM((layers, 2, 32, width), F32),
        dma((10,)),
        dma((10,)),
        dma((10,)),
        dma((2, 2)),
        dma((2, 2)),
        dma((8, 2)),
        dma((8, 2)),
        dma((pieces,)),
        dma((pieces,)),
        dma((pieces, 6)),
        dma((pieces, 6)),
        dma((5,)),
        dma((5,)),
        dma((7,)),
        dma((7,)),
        dma((pieces + 3,)),
        pltpu.SemaphoreType.REGULAR,
    ]
    sums, shared, encoded, grad_patches = pl.pallas_call(
        functools.partial(encoder, wide_count),
        out_shape=(
            jax.ShapeDtypeStruct((layers, per_layer, width), BF),
            jax.ShapeDtypeStruct((2, shared_rows, width), BF),
            jax.ShapeDtypeStruct((local, width), F32),
            jax.ShapeDtypeStruct((local, patch), F32),
        ),
        in_specs=[anyw, anyw, vmem, anyw, vmem, vmem, anyw, vmem, vmem, anyw, vmem, anyw, vmem, anyw, vmem, anyw, vmem],
        out_specs=(anyw, anyw, anyw, anyw),
        scratch_shapes=scratch,
        compiler_params=pltpu.CompilerParams(
            collective_id=0, has_side_effects=True, vmem_limit_bytes=63 * 1024 * 1024 + 512 * 1024
        ),
        name="encoder",
    )(
        rows_in,
        cotangent,
        mask_slots,
        projector.reshape(2 * patch, width),
        offsets,
        placeholder.reshape(1, width),
        positions,
        scales,
        shifts,
        attention,
        attn_bias,
        combiner,
        comb_bias,
        expander,
        expand_bias,
        reducer,
        reduce_bias,
    )
    total = sums.astype(F32)
    both = shared.astype(F32)
    grad_expander = total[:, 0:hid]
    grad_reducer = total[:, hid : 2 * hid]
    grad_attention = total[:, 2 * hid : 2 * hid + 3 * cols].reshape(layers, 3, cols, width).transpose(0, 1, 3, 2)
    grad_combiner = total[:, 2 * hid + 3 * cols : 2 * hid + 4 * cols]
    bias = total[:, 2 * hid + 4 * cols :]
    grad_expbias = bias[:, 0, :]
    grad_attnbias = bias[:, 1:3, :cols]
    grad_projector = both[:, 0:patch]
    grad_positions = both[:, patch : patch + local].reshape(seq, width)
    small = both[0, patch + local :]
    return (
        encoded,
        grad_patches,
        grad_projector,
        small[12:14],
        small[14],
        grad_positions,
        small[0:4].reshape(layers, 2, width),
        small[4:8].reshape(layers, 2, width),
        grad_attention,
        grad_attnbias,
        grad_combiner,
        small[8:10],
        grad_expander,
        grad_expbias,
        grad_reducer,
        small[10:12],
    )


def solution(mesh):
    rows = ("wide", "narrow")
    return jax.shard_map(
        functools.partial(per_device, mesh.shape["wide"]),
        mesh=mesh,
        in_specs=(
            P(rows, None),
            P(rows),
            P("wide", None),
            P(),
            P(),
            P(),
            P(),
            P(),
            P(),
            P(None, None, None, "narrow"),
            P(None, None, "narrow"),
            P(None, "narrow", None),
            P(),
            P(None, None, "narrow"),
            P(None, "narrow"),
            P(None, "narrow", None),
            P(),
            P(rows, None),
        ),
        out_specs=(
            P(rows, None),
            P(rows, None),
            P(),
            P(),
            P(),
            P(),
            P(),
            P(),
            P(None, None, None, "narrow"),
            P(None, None, "narrow"),
            P(None, "narrow", None),
            P(),
            P(None, None, "narrow"),
            P(None, "narrow"),
            P(None, "narrow", None),
            P(),
        ),
        check_vma=False,
    )
```

time: 973 us -> 319 us (0.33)
  waiting for transfers between devices: 637 us -> 0 us
  Pallas kernels: 0 us -> 290 us
  blocking collectives: 152 us -> 0 us
  matrix products: 68.6 us -> 0 us
  other arithmetic: 54.3 us -> 2.35 us
  between operations: 16.2 us -> 0.69 us
  local copies, waits for them, and re-layouts: 36.1 us -> 25.6 us
    psum x2 -> x0, waiting for transfers between devices: 491 us -> none  [the longest x1 363 us: per_device(): lax.psum((grad_attention, grad_attnbias, grad_combiner, grad_expander, gr...]
    pallas_call x0 -> x1, Pallas kernels: none -> 290 us  [per_device(): pl.pallas_call(functools.partial(encoder, wide_count), out_shape=(jax.Sha...]
    reduce_scatter x8 -> x0, waiting for transfers between devices: 146 us -> none  [the longest x4 82.4 us: sum_forward(): lax.psum_scatter(term(jnp.int32(0), local_rows * lax.axis_size('narrow'))...]
    psum x2 -> x0, blocking collectives: 81.8 us -> none  [the longest x1 43.3 us: per_device(): lax.psum((grad_scales, grad_shifts, grad_combbias, grad_redbias, grad_pro...]
    all_gather x8 -> x0, blocking collectives: 69.9 us -> none  [the longest x4 35 us: share_grads(): return lax.all_gather(values, 'narrow', axis=0, tiled=True)]
    dot_general x39 -> x0, matrix products: 68.6 us -> none  [the longest x2 16.4 us: per_device(): jnp.dot(second_all, expander[layer], preferred_element_type=jnp.float32)]
    reduce_sum x21 -> x0, other arithmetic: 25.3 us -> none  [the longest x7 11.4 us: norm_params(): return (jnp.sum(grad * hat, axis=0), jnp.sum(grad, axis=0))]
    another operation x17 -> x0, other arithmetic: 14.5 us -> none  [the longest x8 12.6 us: per_device(): jnp.stack([owned[layer][index] for layer in range(layer_count)])]
  transfers between devices with their start and end apart: 10 -> 0, of which waited for: 9 -> 0; matrix products, arithmetic and copies ran while one was open for 5% -> 0% of each run, Pallas kernels for 0% -> 0%
where the time goes in v1:
time: 319 us; the launch traced here: 318 us
  Pallas kernels  290 us (91%)
  local copies, waits for them, and re-layouts  25.6 us (8%)
    pallas_call x1, Pallas kernels, per_device(): pl.pallas_call(functools.partial(encoder, wide_count), out_shape=(jax.Sha...  290 us
    unnamed x12, local copies, waits for them, and re-layouts  6.94 us

profile of v1, /device:TPU:0, one launch (start us, length us, event | category | flops | bytes accessed | tf_op | source)
XLA Modules:
  0.0 318.2 jit_solution(8404857236681858045)
XLA Ops:
  0.6 0.7 compare_convert_fusion
  1.3 1.3 reshape.61.plc_in
  2.6 0.1 broadcast_in_dim.2
  2.7 1.5 pad_maximum_fusion.rows_in
  4.1 4.0 %copy.34.att_in = bf16[2,3,768,192]{3,2,1,0:T(8,128)(2,1)} copy(bf16[2,3,768,192]{2,3,1,0:T(8,128)(2,1)} %param.27) | data formatting | bytes 3538944 | tf_op args[9]
  8.1 289.6 %encoder.1 = (bf16[2,2336,768]{2,1,0:T(8,128)(2,1)}, bf16[2,448,768]{2,1,0:T(8,128)(2,1)}, f32[128,768]{1,0:T(8,128)}, f32[128,256]{1,0:T(8,128)}) custom-call(bf16[128,384]{1,0:T(8,128)(2,1)} %pad_maximum_fusion.rows_in, bf16[128,768]{1,0:T(8,128)(2,1)} %cot_in.1, s32[2,64]{1,0:T(2,128)} %slots_in.1, bf16[512,768]{1,0:T(8,128)(2,1)} %bitcast.16, ...), custom_call_target="tpu_custom_call" | custom-call | tf_op jit(solution)/shard_map/encoder/pallas_call | solution.py:1139
  297.8 0.0 copy-start.1
  297.8 1.4 slice.88
  299.2 0.7 slice.92
  299.9 0.6 copy.37
  300.5 0.8 fusion.1
  301.3 0.6 reshape.64
  301.9 0.6 reshape.63
  302.5 1.9 slice.84
  304.5 2.2 slice.89
  306.6 0.0 copy-done.1
  306.6 0.0 copy-start
  306.6 1.3 slice.81
  307.9 0.2 convert_element_type.11
  308.1 0.6 slice_reduce_fusion
  308.7 0.6 slice_bitcast_fusion
  309.3 0.9 copy-done
  310.2 2.0 slice.87
  312.3 0.0 copy-start.2
  312.3 0.0 copy-start.3
  312.3 4.5 %fusion = (f32[2,768,768]{2,1,0:T(8,128)}, f32[2,768,768]{2,1,0:T(8,128)}) fusion(bf16[2,2336,768]{2,1,0:T(8,128)(2,1)S(1)} %copy-done), kind=kLoop, calls=%fused_computation.7 | loop fusion | bytes 18874368 | tf_op jit(solution)/shard_map/slice | solution.py:1176
  316.8 0.0 copy-done.2
  316.8 0.7 copy.40
  317.6 0.0 copy-done.3
  317.6 0.7 copy.41
Async XLA Ops:
  297.8 8.9 %copy-start.1 = (bf16[2,448,768]{2,1,0:T(8,128)(2,1)S(1)}, bf16[2,448,768]{2,1,0:T(8,128)(2,1)}, u32[]{:S(2)}) copy-start(bf16[2,448,768]{2,1,0:T(8,128)(2,1)} %get-tuple-element.22) | copy-start | bytes 4128772
  306.6 3.6 %copy-start = (bf16[2,2336,768]{2,1,0:T(8,128)(2,1)S(1)}, bf16[2,2336,768]{2,1,0:T(8,128)(2,1)}, u32[]{:S(2)}) copy-start(bf16[2,2336,768]{2,1,0:T(8,128)(2,1)} %get-tuple-element.23) | copy-start | bytes 21528580
  312.3 4.5 %copy-start.2 = (f32[128,768]{1,0:T(8,128)S(1)}, f32[128,768]{1,0:T(8,128)}, u32[]{:S(2)}) copy-start(f32[128,768]{1,0:T(8,128)} %get-tuple-element.47) | copy-start | bytes 1179652
  312.3 5.3 %copy-start.3 = (f32[128,256]{1,0:T(8,128)S(1)}, f32[128,256]{1,0:T(8,128)}, u32[]{:S(2)}) copy-start(f32[128,256]{1,0:T(8,128)} %get-tuple-element.48) | copy-start | bytes 393220

commit v2 on v1

--- a/solution.py
+++ b/solution.py
@@ -104,6 +104,10 @@
 
 
 class PairFirst:
+    @staticmethod
+    def space(rows):
+        return rows // 2 * 3
+
     def __init__(self, place, total, row, rows, buf, at, out, send, recv, store):
         self.place, self.total, self.buf = place, total, buf
         half = rows // 2
@@ -209,6 +213,10 @@
 
 
 class LineFirst:
+    @staticmethod
+    def space(rows):
+        return rows * 2
+
     def __init__(self, place, total, row, rows, buf, at, out, send, recv, store):
         self.place, self.total, self.buf = place, total, buf
         half = rows // 2
@@ -321,9 +329,50 @@
                 self.give_on.wait_send()
 
 
+KINDS = (PairFirst, LineFirst,)
+PLAN = (1, 0, 0, 0, 0, 0, 1, 1, 0, 1, 0, 0, 0, 0, 0, 1, 0, 0, 0, 0, 1, 1, 0, 1)
+TICKS = (
+    (),
+    (),
+    (),
+    (),
+    (),
+    (),
+    (),
+    (),
+    (),
+    ((1, 1), (0, 1), (2, 1), (3, 1)),
+    ((6, 1),),
+    ((4, 1),),
+    (),
+    (),
+    ((5, 1), (0, 2)),
+    ((7, 1), (6, 2), (8, 1), (1, 2)),
+    ((10, 1), (2, 2), (11, 1), (3, 2)),
+    ((7, 2),),
+    ((0, 3),),
+    ((4, 2),),
+    ((1, 3),),
+    ((6, 3),),
+    (),
+    (),
+    ((2, 3), (12, 1)),
+    ((9, 1), (3, 3), (7, 3), (1, 4), (5, 2), (0, 4), (13, 1)),
+    ((8, 2), (4, 3)),
+    ((14, 1),),
+    ((2, 4), (10, 2)),
+    ((6, 4),),
+    (),
+    ((3, 4), (11, 2), (9, 2), (16, 1), (7, 4), (17, 1)),
+    ((0, 5), (15, 1)),
+    ((5, 3), (1, 5), (18, 1), (4, 4), (12, 2), (8, 3), (19, 1), (6, 5), (13, 2), (10, 3), (2, 5), (7, 5), (11, 3), (3, 5), (5, 4), (20, 1), (15, 2), (8, 4), (14, 2), (12, 3), (4, 5), (22, 1), (10, 4), (13, 3), (9, 3), (11, 4), (21, 1), (20, 2), (24, 1), (12, 4), (14, 3), (5, 5), (13, 4), (23, 1), (9, 4), (8, 5), (16, 2), (21, 2), (10, 5), (14, 4), (17, 2), (23, 2), (11, 5), (9, 5), (18, 2), (16, 3), (15, 3), (19, 2), (17, 3), (12, 5), (22, 2), (16, 4), (18, 3), (13, 5), (24, 2), (15, 4), (20, 3), (17, 4), (19, 3), (14, 5), (18, 4), (22, 3), (21, 3), (15, 5), (24, 3), (23, 3), (20, 4), (16, 5), (19, 4), (21, 4), (17, 5), (22, 4), (23, 4), (18, 5), (19, 5), (24, 4), (22, 5), (24, 5), (20, 5), (21, 5), (23, 5), (24, 6), (24, 7)),
+)
+
+
 def encoder(
     wide_count,
-    rows_in,
+    patches_in,
+    kinds_in,
     cot_in,
     slots_in,
     proj_in,
@@ -353,6 +402,8 @@
     proj,
     pos,
     rows_all,
+    kinds_all,
+    flags,
     grad,
     stream,
     middle,
@@ -411,7 +462,7 @@
     patch = proj_in.shape[0] // 2
     seq = pos_in.shape[0]
     layers = scales.shape[0]
-    cols = att_in.shape[3]
+    cols = att_in.shape[2]
     heads = cols // HD
     hid = exp_in.shape[2]
     scale = HD ** (-0.5)
@@ -440,7 +491,9 @@
     near = (w, 3 * y)
     here = span(c, local)
     row_copies = []
-    for k, (src, dst) in enumerate(((rows_in, rows_all), (cot_in, cot))):
+    for k, (src, dst, here) in enumerate(
+        ((patches_in, rows_all, here), (cot_in, cot, here), (kinds_in, kinds_all, pl.ds(c, 1)))
+    ):
         row_copies.append(
             (
                 Copy(src, dst.at[here], rows_send.at[k, 0], rows_recv.at[k, c], far),
@@ -461,12 +514,13 @@
         def _():
             to_near.start()
 
-    def wait_rows(k, dst):
+    def wait_rows(k, dst, size):
         for h in range(2):
-            spot = dst.at[pl.ds(h * local, local)]
+            spot = dst.at[pl.ds(h * size, size)]
             pltpu.make_async_copy(spot, spot, rows_recv.at[k, h]).wait()
 
     send_rows(0)
+    send_rows(2)
     weights = []
     for layer in range(layers):
         for src, dst in ((att_in, wa), (comb_in, wc), (exp_in, we), (red_in, wr)):
@@ -525,18 +579,21 @@
     place_col = lax.broadcasted_iota(jnp.int32, (seq, slots_in.shape[1]), 0)
     slot_row = slots_in[pl.ds(c, 1), :]
     masked = jnp.max(jnp.where(place_col == slot_row, 1.0, 0.0).astype(F32), axis=1, keepdims=True)
-    wait_rows(0, rows_all)
+    wait_rows(0, rows_all, local)
+    wait_rows(2, kinds_all, 1)
+    for h in range(2):
+        kinds = jnp.broadcast_to(jnp.where(kinds_all[h : h + 1, :] == 1, 1.0, 0.0), (128, 128)).astype(F32)
+        flags[pl.ds(h * local, local), :] = kinds.T.astype(BF)
     proj_load.wait()
     pos_load.wait()
-    flags = rows_all[:, patch : patch + 128]
-    wide_flags = jnp.concatenate([flags] * (patch // 128), axis=1)
-    patches = rows_all[:, :patch]
+    wide_flags = jnp.concatenate([flags[...]] * (patch // 128), axis=1)
+    patches = rows_all[...]
     kind_one = patches * wide_flags
     kind_zero = patches - kind_one
     is_one = flags[:, 0:1].astype(F32)
     lifted = nn(kind_zero, proj[0:patch, :]) + nn(kind_one, proj[patch : 2 * patch, :])
     offset = jnp.where(is_one > 0.5, offs_in[1:2, :].astype(F32), offs_in[0:1, :].astype(F32))
-    stream[0] = jnp.where(masked > 0.5, plc_in[...].astype(F32), lifted + offset) + pos[...].astype(F32)
+    stream[0] = jnp.where(masked > 0.5, plc_in[...].reshape(1, width).astype(F32), lifted + offset) + pos[...].astype(F32)
 
     def before_attention(layer):
         def norm(ch):
@@ -554,10 +611,10 @@
 
         def group(g):
             rows = first[layer]
-            query = (nn(rows, wa[layer, g, 0]) + abias[g, layer, 0:1, :].astype(F32)) * scale
+            query = (nt(rows, wa[layer, g, 0]) + abias[g, layer, 0:1, :].astype(F32)) * scale
             qkv[layer, g, 0] = query.astype(BF)
-            qkv[layer, g, 1] = nn(rows, wa[layer, g, 1]).astype(BF)
-            qkv[layer, g, 2] = (nn(rows, wa[layer, g, 2]) + abias[g, layer, 1:2, :].astype(F32)).astype(BF)
+            qkv[layer, g, 1] = nt(rows, wa[layer, g, 1]).astype(BF)
+            qkv[layer, g, 2] = (nt(rows, wa[layer, g, 2]) + abias[g, layer, 1:2, :].astype(F32)).astype(BF)
 
         loop(2, group)
 
@@ -649,105 +706,106 @@
             loop(chunks, after)
 
     pieces = []
-    base = 0
     at = 0
-    plan = (
-        (PairFirst, 0, hid // 2),
-        (PairFirst, hid // 2, hid // 2),
-        (LineFirst, hid, hid // 2),
-        (LineFirst, hid + hid // 2, hid // 2),
-        (PairFirst, 2 * hid, 2 * cols),
-        (PairFirst, 2 * hid + 2 * cols, cols),
-        (LineFirst, 2 * hid + 3 * cols, cols + 32),
-    )
-    per_layer = len(plan)
+    cut = hid // 4
+    spots = [(hid + (k // 2) * cut if k % 2 == 0 else (k // 2) * cut, cut) for k in range(8)]
+    spots += [(2 * hid + j * cols, cols) for j in range(3)] + [(2 * hid + 3 * cols, cols + 32)]
+    per_layer = len(spots)
     for layer in reversed(range(layers)):
-        for kind, row, count in plan:
+        for row, count in spots:
             k = len(pieces)
-            pieces.append((kind(place, total.at[layer], row, count, ring, at, sums_out.at[layer], ring_send.at[k], ring_recv.at[k], store_sem.at[k]), layer, row, count))
-            at += count // 2 * 3 if kind is PairFirst else count * 2
-
-    def parts(k, own, other):
-        piece, layer, row, count = pieces[k]
-        slot = k % 2
-        copy = Copy(
-            send_part.at[slot, pl.ds(0, count)], recv_part.at[pl.ds(row, count)], part_send.at[k], part_recv.at[k], sibling
+            kind = KINDS[PLAN[k]]
+            piece = kind(
+                place,
+                total.at[layer],
+                row,
+                count,
+                ring,
+                at,
+                sums_out.at[layer],
+                ring_send.at[k],
+                ring_recv.at[k],
+                store_sem.at[k],
+            )
+            pieces.append((piece, layer, row, count))
+            at += kind.space(count)
+
+    def part_copy(k):
+        _, _, row, count = pieces[k]
+        return Copy(
+            send_part.at[k % 4, pl.ds(0, count)],
+            recv_part.at[pl.ds(row, count)],
+            part_send.at[k],
+            part_recv.at[k],
+            sibling,
         )
-        if k >= 2:
-            old = pieces[k - 2]
-            Copy(
-                send_part.at[slot, pl.ds(0, old[3])],
-                recv_part.at[pl.ds(old[2], old[3])],
-                part_send.at[k - 2],
-                part_recv.at[k - 2],
-                sibling,
-            ).wait_send()
+
+    def begin(k, own, other):
+        _, layer, row, count = pieces[k]
+        if k >= 4:
+            part_copy(k - 4).wait_send()
         if k == per_layer:
             pl.semaphore_wait(credit, 1)
-        other(send_part.at[slot])
-        copy.start()
+        other(send_part.at[k % 4])
+        part_copy(k).start()
         own(total.at[layer, pl.ds(row, count)])
-        copy.wait_recv()
+
+    def join(k):
+        piece, layer, row, count = pieces[k]
+        part_copy(k).wait_recv()
         add_into(total.at[layer], row, recv_part, row, count)
         if k == per_layer - 1:
             pl.semaphore_signal(credit, 1, device_id=sibling, device_id_type=MESH)
         piece.stages[0]()
 
-    done = {}
-
-    def advance(k):
-        stage = done.get(k, 1)
-        if stage < 6:
-            pieces[k][0].stages[stage]()
-        done[k] = stage + 1
-
-    def weight_grad(left, right, g):
-        count = left.shape[1] // 128
-
+    ticks = iter(TICKS)
+
+    def tick():
+        for k, stage in next(ticks):
+            (pieces[k][0] if k < len(pieces) else shared_piece[0]).stages[stage]()
+
+    shared_piece = []
+
+    def weight_grad(left, right):
         def into(ref):
-            def step(t):
-                ref[span(t, 128), :] = tn(left[:, span(t, 128)], right).astype(BF)
-
-            loop(count, step)
+            ref[pl.ds(0, left.shape[1]), :] = tn(left[...], right[...]).astype(BF)
 
         return into
 
+    def run_pieces(base, works):
+        for i, (own, other) in enumerate(works):
+            begin(base + i, own, other)
+            if i > 0:
+                join(base + i - 1)
+                tick()
+        join(base + len(works) - 1)
+        tick()
+
     def feed_grads(layer, base):
-        for t in range(2):
-            cut = pl.ds(t * (hid // 2), hid // 2)
-            parts(
-                base + t,
-                weight_grad(second.at[layer, :, cut], pre[0], 0),
-                weight_grad(second.at[layer, :, cut], pre[1], 1),
-            )
-        for t in range(2):
-            cut = pl.ds(t * (hid // 2), hid // 2)
-            parts(
-                base + 2 + t,
-                weight_grad(hidden.at[layer, 0, :, cut], out_round[...], 0),
-                weight_grad(hidden.at[layer, 1, :, cut], out_round[...], 1),
-            )
+        works = []
+        for k in range(8):
+            lanes = pl.ds((k // 2) * cut, cut)
+            if k % 2 == 0:
+                works.append([weight_grad(hidden.at[layer, g, :, lanes], out_round) for g in range(2)])
+            else:
+                works.append([weight_grad(second.at[layer, :, lanes], pre.at[g]) for g in range(2)])
+        run_pieces(base, works)
 
     def attention_grads(layer, base):
-        def stack(g, which):
+        def comb(g):
+            grad_comb = weight_grad(mixed.at[layer, g], mid_round)
+
             def into(ref):
-                for j, index in enumerate(which):
-                    ref[pl.ds(j * cols, cols), :] = tn(grad_qkv[g, index], first[layer]).astype(BF)
+                grad_comb(ref)
+                ref[pl.ds(cols, 32), :] = bias_rows[layer, g].astype(BF)
 
             return into
 
-        def comb(g):
-            def into(ref):
-                ref[pl.ds(0, cols), :] = tn(mixed[layer, g], mid_round[...]).astype(BF)
-                ref[pl.ds(cols, 32), :] = bias_rows[layer, g].astype(BF)
-
-            return into
-
-        parts(base + 4, stack(0, (0, 1)), stack(1, (0, 1)))
-        parts(base + 5, stack(0, (2,)), stack(1, (2,)))
-        parts(base + 6, comb(0), comb(1))
-
-    wait_rows(1, cot)
+        works = [[weight_grad(grad_qkv.at[g, j], first.at[layer]) for g in range(2)] for j in range(3)]
+        works.append([comb(g) for g in range(2)])
+        run_pieces(base + 8, works)
+
+    wait_rows(1, cot, local)
     last = layers - 1
 
     def start_back(ch):
@@ -790,6 +848,7 @@
             offer(exchange, 1, ch, acc[...])
 
         loop(chunks, chunk)
+        tick()
 
         if layer == last:
 
@@ -848,6 +907,7 @@
             loop(2, group)
 
         loop(chunks, chunk)
+        tick()
 
         def close(g):
             grad_qkv[g, 1] = key_acc[g, 0].astype(BF)
@@ -862,9 +922,9 @@
 
             def group(g):
                 part = (
-                    nt(grad_qkv[g, 0, rows, :], wa[layer, g, 0])
-                    + nt(grad_qkv[g, 1, rows, :], wa[layer, g, 1])
-                    + nt(grad_qkv[g, 2, rows, :], wa[layer, g, 2])
+                    nn(grad_qkv[g, 0, rows, :], wa[layer, g, 0])
+                    + nn(grad_qkv[g, 1, rows, :], wa[layer, g, 1])
+                    + nn(grad_qkv[g, 2, rows, :], wa[layer, g, 2])
                 )
 
                 @pl.when(g == 0)
@@ -879,6 +939,7 @@
             offer(exchange + 1, 0, ch, acc[...])
 
         loop(chunks, chunk)
+        tick()
         attention_grads(layer, base)
 
         if layer == last:
@@ -909,6 +970,7 @@
             grad[rows, :] += settle(rows, layer, 0, stream[layer, rows, :], grad_first, None)
 
         loop(chunks, chunk)
+        tick()
 
     lifted_grad = jnp.where(masked > 0.5, 0.0, grad[...])
     note(14, grad[...] - lifted_grad)
@@ -919,7 +981,7 @@
     shared_rows = shared.shape[0]
     half_rows = shared_rows // 2
     flag_side = jnp.where(y == 1, wide_flags.astype(F32), 1.0 - wide_flags.astype(F32)).astype(BF)
-    shared[0:patch, :] = tn(rows_all[:, :patch] * flag_side, lifted_round).astype(BF)
+    shared[0:patch, :] = tn(rows_all[...] * flag_side, lifted_round).astype(BF)
     shared[patch : patch + local, :] = grad[span(y, local), :].astype(BF)
     shared[patch + local : shared_rows, :] = small[...].astype(BF)
     keep_row, give_row = span(c, half_rows), span(1 - c, half_rows)
@@ -934,7 +996,7 @@
     def _():
         def half_back(dst, half):
             rows = span(half, local)
-            flag = rows_all[rows, patch : patch + 128].astype(F32)[:, 0:1]
+            flag = flags[rows, :].astype(F32)[:, 0:1]
             masks = jnp.max(
                 jnp.where(
                     lax.broadcasted_iota(jnp.int32, (local, slots_in.shape[1]), 0) + half * local == slot_row, 1.0, 0.0
@@ -951,7 +1013,7 @@
 
     shared_part.wait()
     add_into(shared, pl.multiple_of(c * half_rows, 16), shared_buf, 0, half_rows)
-    shared_piece = PairFirst(
+    sum_shared = PairFirst(
         place,
         shared,
         pl.multiple_of(c * half_rows, 16),
@@ -963,23 +1025,10 @@
         shared_recv,
         store_sem.at[len(pieces)],
     )
-    shared_piece.stages[0]()
-
-    count = len(pieces)
-    for stage in range(1, 5):
-        shared_piece.stages[stage]()
-        for k in range(count):
-            advance(k)
-    shared_piece.stages[5]()
     across = Copy(shared_out.at[y, keep_row], shared_out.at[y, keep_row], last_send.at[4], last_recv.at[4], partner)
     across_back = Copy(
         shared_out.at[1 - y, keep_row], shared_out.at[1 - y, keep_row], last_send.at[4], last_recv.at[4], partner
     )
-    across.start()
-    for k in range(count):
-        advance(k)
-    across.wait_send()
-    across_back.wait_recv()
     ends = []
     for k in range(2):
         ends.append(
@@ -992,11 +1041,28 @@
                 ),
             )
         )
-    for out, _ in ends:
-        out.start()
-    for out, back in ends:
-        out.wait_send()
-        back.wait_recv()
+
+    def to_partner():
+        sum_shared.s5()
+        across.start()
+
+    def to_sibling():
+        across.wait_send()
+        across_back.wait_recv()
+        for out, _ in ends:
+            out.start()
+
+    def close_shared():
+        for out, back in ends:
+            out.wait_send()
+            back.wait_recv()
+
+    sum_shared.stages = sum_shared.stages[:5] + [to_partner, to_sibling, close_shared]
+    shared_piece.append(sum_shared)
+    sum_shared.s0()
+    tick()
+    tick()
+    count = len(pieces)
 
     @pl.when(diagonal)
     def _():
@@ -1026,15 +1092,8 @@
 
     for copy in sib_loads + [abias_copy, ebias_copy]:
         copy.wait_send()
-    for k in (count - 2, count - 1):
-        piece, layer, row, size = pieces[k]
-        Copy(
-            send_part.at[k % 2, pl.ds(0, size)],
-            recv_part.at[pl.ds(row, size)],
-            part_send.at[k],
-            part_recv.at[k],
-            sibling,
-        ).wait_send()
+    for k in range(count - 4, count):
+        part_copy(k).wait_send()
 
 
 def per_device(
@@ -1064,19 +1123,16 @@
     cols = attention.shape[3]
     heads = cols // HD
     hid = expander.shape[2]
-    flags = jnp.broadcast_to((token_kind == 1)[:, None], (local, 128)).astype(BF)
-    rows_in = jnp.concatenate([patches, flags], axis=1)
     per_layer = 2 * hid + 4 * cols + 32
     shared_rows = patch + local + 64
-    pieces = 7 * layers
-    ring_rows = layers * (
-        3 * (hid // 2) + 3 * cols + 3 * (cols // 2) + 2 * hid + 2 * (cols + 32)
-    )
+    pieces = 12 * layers
+    counts = ([hid // 4] * 8 + [cols] * 3 + [cols + 32]) * layers
+    ring_rows = sum(KINDS[kind].space(count) for kind, count in zip(PLAN, counts))
     vmem = pl.BlockSpec(memory_space=pltpu.VMEM)
     anyw = pl.BlockSpec(memory_space=pl.ANY)
     dma = pltpu.SemaphoreType.DMA
     scratch = [
-        pltpu.VMEM((layers, 2, 3, width, cols), BF),
+        pltpu.VMEM((layers, 2, 3, cols, width), BF),
         pltpu.VMEM((layers, 2, cols, width), BF),
         pltpu.VMEM((layers, 2, width, hid), BF),
         pltpu.VMEM((layers, 2, hid, width), BF),
@@ -1084,7 +1140,9 @@
         pltpu.VMEM((2, layers, hid), BF),
         pltpu.VMEM((2 * patch, width), BF),
         pltpu.VMEM((seq, width), BF),
-        pltpu.VMEM((seq, patch + 128), BF),
+        pltpu.VMEM((seq, patch), BF),
+        pltpu.VMEM((2, local), jnp.int32),
+        pltpu.VMEM((seq, 128), BF),
         pltpu.VMEM((seq, width), F32),
         pltpu.VMEM((layers, seq, width), F32),
         pltpu.VMEM((layers, seq, width), F32),
@@ -1106,7 +1164,7 @@
         pltpu.VMEM((2, seq, width), BF),
         pltpu.VMEM((seq, width), BF),
         pltpu.VMEM((seq, width), BF),
-        pltpu.VMEM((2, 2 * cols, width), BF),
+        pltpu.VMEM((4, cols + 32, width), BF),
         pltpu.VMEM((per_layer, width), BF),
         pltpu.VMEM((layers, per_layer, width), BF),
         pltpu.VMEM((ring_rows, width), BF),
@@ -1121,8 +1179,8 @@
         dma((10,)),
         dma((10,)),
         dma((10,)),
-        dma((2, 2)),
-        dma((2, 2)),
+        dma((3, 2)),
+        dma((3, 2)),
         dma((8, 2)),
         dma((8, 2)),
         dma((pieces,)),
@@ -1144,7 +1202,7 @@
             jax.ShapeDtypeStruct((local, width), F32),
             jax.ShapeDtypeStruct((local, patch), F32),
         ),
-        in_specs=[anyw, anyw, vmem, anyw, vmem, vmem, anyw, vmem, vmem, anyw, vmem, anyw, vmem, anyw, vmem, anyw, vmem],
+        in_specs=[anyw, vmem, anyw, vmem, anyw, vmem, vmem, anyw, vmem, vmem, anyw, vmem, anyw, vmem, anyw, vmem, anyw, vmem],
         out_specs=(anyw, anyw, anyw, anyw),
         scratch_shapes=scratch,
         compiler_params=pltpu.CompilerParams(
@@ -1152,16 +1210,17 @@
         ),
         name="encoder",
     )(
-        rows_in,
+        patches,
+        token_kind.reshape(1, local),
         cotangent,
         mask_slots,
         projector.reshape(2 * patch, width),
         offsets,
-        placeholder.reshape(1, width),
+        placeholder,
         positions,
         scales,
         shifts,
-        attention,
+        attention.transpose(0, 1, 3, 2),
         attn_bias,
         combiner,
         comb_bias,
@@ -1170,36 +1229,150 @@
         reducer,
         reduce_bias,
     )
-    total = sums.astype(F32)
-    both = shared.astype(F32)
-    grad_expander = total[:, 0:hid]
-    grad_reducer = total[:, hid : 2 * hid]
-    grad_attention = total[:, 2 * hid : 2 * hid + 3 * cols].reshape(layers, 3, cols, width).transpose(0, 1, 3, 2)
-    grad_combiner = total[:, 2 * hid + 3 * cols : 2 * hid + 4 * cols]
-    bias = total[:, 2 * hid + 4 * cols :]
-    grad_expbias = bias[:, 0, :]
-    grad_attnbias = bias[:, 1:3, :cols]
-    grad_projector = both[:, 0:patch]
-    grad_positions = both[:, patch : patch + local].reshape(seq, width)
-    small = both[0, patch + local :]
-    return (
-        encoded,
-        grad_patches,
-        grad_projector,
-        small[12:14],
-        small[14],
-        grad_positions,
-        small[0:4].reshape(layers, 2, width),
-        small[4:8].reshape(layers, 2, width),
-        grad_attention,
-        grad_attnbias,
-        grad_combiner,
-        small[8:10],
-        grad_expander,
-        grad_expbias,
-        grad_reducer,
-        small[10:12],
-    )
+    f32 = functools.partial(jax.ShapeDtypeStruct, dtype=F32)
+    finished = pl.pallas_call(
+        widen,
+        out_shape=(
+            f32((local, width)),
+            f32((local, patch)),
+            f32((2, patch, width)),
+            f32((2, width)),
+            f32((width,)),
+            f32((seq, width)),
+            f32((layers, 2, width)),
+            f32((layers, 2, width)),
+            f32((layers, 3, cols, width)),
+            f32((layers, 2, cols)),
+            f32((layers, cols, width)),
+            f32((layers, width)),
+            f32((layers, width, hid)),
+            f32((layers, hid)),
+            f32((layers, hid, width)),
+            f32((layers, width)),
+        ),
+        in_specs=[anyw] * 4,
+        out_specs=[anyw, anyw, anyw, vmem, vmem, anyw, vmem, vmem, anyw, vmem, anyw, vmem, anyw, vmem, anyw, vmem],
+        scratch_shapes=[
+            pltpu.VMEM((layers, per_layer, width), BF),
+            pltpu.VMEM((layers, per_layer - 32, width), F32),
+            pltpu.VMEM((2, shared_rows, width), BF),
+            pltpu.VMEM((2, patch + local, width), F32),
+            pltpu.VMEM((local, width), F32),
+            pltpu.VMEM((local, patch), F32),
+            dma((layers, 4)),
+            dma((layers, 6)),
+            dma((2,)),
+            dma((2, 2)),
+            dma((2, 2)),
+        ],
+        compiler_params=pltpu.CompilerParams(vmem_limit_bytes=62 * 1024 * 1024),
+        name="widen",
+    )(sums, shared, encoded, grad_patches)
+    return tuple(item.transpose(0, 1, 3, 2) if k == 8 else item for k, item in enumerate(finished))
+
+
+def widen(
+    sums,
+    shared,
+    encoded,
+    grad_patches,
+    encoded_out,
+    patches_out,
+    projector,
+    offsets,
+    placeholder,
+    positions,
+    scales,
+    shifts,
+    attention,
+    attn_bias,
+    combiner,
+    comb_bias,
+    expander,
+    expand_bias,
+    reducer,
+    reduce_bias,
+    sums_in,
+    sums_wide,
+    shared_in,
+    shared_wide,
+    encoded_held,
+    patches_held,
+    load_sem,
+    store_sem,
+    shared_sem,
+    shared_store,
+    through_sem,
+):
+    layers, width, hid = expander.shape
+    cols = combiner.shape[1]
+    patch = projector.shape[1]
+    local = encoded.shape[0]
+    through = [
+        (pltpu.make_async_copy(src, held, through_sem.at[k, 0]), pltpu.make_async_copy(held, dst, through_sem.at[k, 1]))
+        for k, (src, held, dst) in enumerate(
+            ((encoded, encoded_held, encoded_out), (grad_patches, patches_held, patches_out))
+        )
+    ]
+    tail = sums.shape[1] - 3 * cols - 2 * hid
+    cuts = ((0, hid), (hid, hid), (2 * hid, 3 * cols), (2 * hid + 3 * cols, tail))
+    loads = []
+    for layer in range(layers):
+        for k, (row, count) in enumerate(cuts):
+            spot = (layer, pl.ds(row, count))
+            loads.append(pltpu.make_async_copy(sums.at[spot], sums_in.at[spot], load_sem.at[layer, k]))
+    shared_loads = [pltpu.make_async_copy(shared.at[k], shared_in.at[k], shared_sem.at[k]) for k in range(2)]
+    for copy in loads + shared_loads + [load for load, _ in through]:
+        copy.start()
+    stores = []
+
+    def convert(src, dst, row, count):
+        def step(t):
+            rows = pl.ds(pl.multiple_of(row + t * 64, 64), 64)
+            dst[rows, :] = src[rows, :].astype(F32)
+
+        loop(count // 64, step)
+
+    for layer in range(layers):
+        for k, (row, count) in enumerate(cuts):
+            loads[layer * len(cuts) + k].wait()
+            wide = min(count, sums_wide.shape[1] - row)
+            convert(sums_in.at[layer], sums_wide.at[layer], row, wide)
+            if k == 2:
+                targets = [(attention.at[layer, j], row + j * cols, cols, 2 + j) for j in range(3)]
+            else:
+                targets = [((expander, reducer, None, combiner)[k].at[layer], row, wide, (0, 1, None, 5)[k])]
+            for target, start, size, sem in targets:
+                copy = pltpu.make_async_copy(sums_wide.at[layer, pl.ds(start, size)], target, store_sem.at[layer, sem])
+                copy.start()
+                stores.append(copy)
+        bias = sums_in[layer, pl.ds(2 * hid + 4 * cols, 16), :].astype(F32)
+        expand_bias[layer : layer + 1, :] = bias[0:1, :]
+        attn_bias[layer, 0:1, :] = bias[1:2, :cols]
+        attn_bias[layer, 1:2, :] = bias[2:3, :cols]
+    for k in range(2):
+        shared_loads[k].wait()
+        convert(shared_in.at[k], shared_wide.at[k], 0, patch + local)
+        for target, start, size, sem in (
+            (projector.at[k], 0, patch, 0),
+            (positions.at[pl.ds(k * local, local)], patch, local, 1),
+        ):
+            copy = pltpu.make_async_copy(shared_wide.at[k, pl.ds(start, size)], target, shared_store.at[k, sem])
+            copy.start()
+            stores.append(copy)
+    for load, store in through:
+        load.wait()
+        store.start()
+    small = shared_in[0, pl.ds(patch + local, 16), :].astype(F32)
+    for layer in range(layers):
+        scales[layer] = small[2 * layer : 2 * layer + 2, :]
+        shifts[layer] = small[4 + 2 * layer : 6 + 2 * layer, :]
+    comb_bias[...] = small[8:10, :]
+    reduce_bias[...] = small[10:12, :]
+    offsets[...] = small[12:14, :]
+    placeholder[...] = small[14:15, :].reshape(width)
+    for copy in stores + [store for _, store in through]:
+        copy.wait()
 
 
 def solution(mesh):

time: 319 us -> 213 us (0.67)
  Pallas kernels: 290 us -> 212 us
  local copies, waits for them, and re-layouts: 25.6 us -> 0 us
    pallas_call x1, Pallas kernels: 290 us -> 203 us  [per_device(): pl.pallas_call(functools.partial(encoder, wide_count), out_shape=(jax.Sha...]
    slice x10 -> x0, local copies, waits for them, and re-layouts: 16 us -> none  [the longest x1 4.53 us: per_device(): grad_reducer = total[:, hid:2 * hid]]
    pallas_call x0 -> x1, Pallas kernels: none -> 9.09 us  [per_device(): pl.pallas_call(widen, out_shape=(f32((local, width)), f32((local, patch))...]
    unnamed x12 -> x0, local copies, waits for them, and re-layouts: 6.94 us -> none
where the time goes in v2:
time: 213 us
  Pallas kernels  212 us (100%)
    pallas_call x1, Pallas kernels, per_device(): pl.pallas_call(functools.partial(encoder, wide_count), out_shape=(jax.Sha...  203 us
    pallas_call x1, Pallas kernels, per_device(): pl.pallas_call(widen, out_shape=(f32((local, width)), f32((local, patch))...  9.09 us

profile of v2, /device:TPU:0, one launch (start us, length us, event | category | flops | bytes accessed | tf_op | source)
XLA Modules:
  0.0 213.1 jit_solution(13920565907624498665)
XLA Ops:
  0.7 203.2 %encoder.1 = (bf16[2,2336,768]{2,1,0:T(8,128)(2,1)}, bf16[2,448,768]{2,1,0:T(8,128)(2,1)}, f32[128,768]{1,0:T(8,128)}, f32[128,256]{1,0:T(8,128)}) custom-call(bf16[128,256]{1,0:T(8,128)(2,1)} %patches_in.1, s32[1,128]{1,0:T(1,128)} %bitcast.6, bf16[128,768]{1,0:T(8,128)(2,1)} %cot_in.1, s32[2,64]{1,0:T(2,128)} %slots_in.1, bf16[512,768]{1,0:T(8,128)(2,1)} %bitcast.5, ...), custom_call_target="tpu_custom_call" | custom-call | tf_op jit(solution)/shard_map/encoder/pallas_call | solution.py:1197
  203.9 9.1 %widen.1 = (f32[128,768]{1,0:T(8,128)}, f32[128,256]{1,0:T(8,128)}, f32[2,256,768]{2,1,0:T(8,128)}, f32[2,768]{1,0:T(2,128)}, f32[768]{0:T(1024)}, /*index=5*/f3...) custom-call(bf16[2,2336,768]{2,1,0:T(8,128)(2,1)} %get-tuple-element, ...), custom_call_target="tpu_custom_call" | custom-call | tf_op jit(solution)/shard_map/widen/pallas_call | solution.py:1233

commit v3 on v2

--- a/solution.py
+++ b/solution.py
@@ -212,125 +212,150 @@
         self.other.wait_recv()
 
 
-class LineFirst:
+class LineScatter:
     @staticmethod
     def space(rows):
-        return rows * 2
+        return rows // 4 * 7
 
     def __init__(self, place, total, row, rows, buf, at, out, send, recv, store):
-        self.place, self.total, self.buf = place, total, buf
-        half = rows // 2
-        self.row, self.rows, self.half, self.at = row, rows, half, at
-        mine = pl.multiple_of(row + place.side * half, 16)
-        other = pl.multiple_of(row + (1 - place.side) * half, 16)
+        quarter = rows // 4
+        self.place, self.total, self.row, self.quarter = place, total, row, quarter
+        self.buf, self.at = buf, at
+        mine = pl.multiple_of(row + place.z * quarter, 16)
         self.mine = mine
-        whole = total.at[pl.ds(row, rows)]
-        keep, give = total.at[pl.ds(mine, half)], total.at[pl.ds(other, half)]
-        out_keep, out_give = out.at[pl.ds(mine, half)], out.at[pl.ds(other, half)]
-        self.line_in = Copy(whole, buf.at[pl.ds(at, rows)], send.at[0], recv.at[0], place.inward)
-        self.middle = Copy(give, buf.at[pl.ds(at + rows, half)], send.at[1], recv.at[1], place.inward)
-        self.across = Copy(keep, buf.at[pl.ds(at + rows + half, half)], send.at[2], recv.at[2], place.pair)
-        self.middle_out = Copy(keep, out_keep, send.at[3], recv.at[3], place.inward)
-        self.middle_back = Copy(out_give, out_give, send.at[3], recv.at[3], place.inward)
-        self.keep_out = Copy(keep, out_keep, send.at[4], recv.at[4], place.outward)
-        self.keep_on = Copy(out_keep, out_keep, send.at[4], recv.at[4], place.outward)
-        self.give_on = Copy(out_give, out_give, send.at[5], recv.at[5], place.outward)
-        self.store = pltpu.make_async_copy(keep, out_keep, store)
-        self.stages = [self.s0, self.s1, self.s2, self.s3, self.s4, self.s5]
+        low, high = (place.w - 2, place.n), (place.w + 2, place.n)
+
+        def own(start, stop):
+            return total.at[pl.ds(row + start * quarter, (stop - start) * quarter)]
+
+        def slot(start, count):
+            return buf.at[pl.ds(at + start * quarter, count * quarter)]
+
+        self.up = [Copy(own(z + 1, 4), slot(z, 3 - z), send.at[0], recv.at[0], high) for z in range(3)]
+        self.down = [Copy(own(0, z), slot(3, z), send.at[1], recv.at[1], low) for z in range(4)]
+        keep, land = total.at[pl.ds(mine, quarter)], out.at[pl.ds(mine, quarter)]
+        self.across = Copy(keep, slot(6, 1), send.at[2], recv.at[2], place.pair)
+        self.store = pltpu.make_async_copy(keep, land, store)
+
+        def spread(src, dst, k, target, way):
+            return Copy(src, dst, send.at[3 + 4 * way + k], recv.at[3 + k], target)
+
+        spots = [out.at[pl.ds(row + k * quarter, quarter)] for k in range(4)]
+        self.first_up = [spread(own(k, k + 1), spots[k], k, high, 0) for k in range(4)]
+        self.first_down = [spread(own(k, k + 1), spots[k], k, low, 1) for k in range(4)]
+        self.on_up = [spread(spots[k], spots[k], k, high, 0) for k in range(4)]
+        self.on_down = [spread(spots[k], spots[k], k, low, 1) for k in range(4)]
+        self.stages = [self.s0, self.s1, self.s2, self.s3, self.s4, self.s5, self.s6, self.s7]
+
+    def at_z(self, *works):
+        for z, work in works:
+            pl.when(self.place.z == z)(work)
+
+    def take(self, copy, first, slot, count):
+        copy.wait_recv()
+        add_into(self.total, self.row + first * self.quarter, self.buf, self.at + slot * self.quarter, count * self.quarter)
 
     def s0(self):
-        place = self.place
-        if place.half == 1:
-            self.middle.start()
-            return
-
-        @pl.when(place.depth == 0)
-        def _():
-            self.line_in.start()
+        self.at_z((0, self.up[0].start), (3, self.down[3].start))
 
     def s1(self):
-        place = self.place
-
-        def hop(k):
-            @pl.when(place.depth == k + 1)
-            def _():
-                self.line_in.wait_recv()
-                add_into(self.total, self.row, self.buf, self.at, self.rows)
-
-            @pl.when((place.depth == k + 1) & jnp.logical_not(place.inner))
-            def _():
-                self.line_in.start()
-
-        hops(place.half - 1, hop)
-        if place.half > 1:
-
-            @pl.when(place.inner)
-            def _():
-                self.middle.start()
+        def one():
+            self.take(self.up[0], 1, 0, 3)
+            self.up[1].start()
+
+        def two():
+            self.take(self.down[3], 0, 3, 3)
+            self.down[2].start()
+
+        self.at_z((1, one), (2, two))
 
     def s2(self):
-        @pl.when(self.place.inner)
-        def _():
-            self.middle.wait()
-            add_into(self.total, self.mine, self.buf, self.at + self.rows, self.half)
-            self.across.start()
+        def one():
+            self.take(self.down[2], 0, 3, 2)
+            self.down[1].start()
+
+        def two():
+            self.take(self.up[1], 2, 1, 2)
+            self.up[2].start()
+
+        self.at_z((1, one), (2, two))
 
     def s3(self):
-        place = self.place
-
-        @pl.when(place.inner)
-        def _():
-            self.across.wait()
-            add_into(self.total, self.mine, self.buf, self.at + self.rows + self.half, self.half)
-            self.middle_out.start()
-            if place.half > 1:
-                self.keep_out.start()
-            self.store.start()
+        self.at_z((0, lambda: self.take(self.down[1], 0, 3, 1)), (3, lambda: self.take(self.up[2], 3, 2, 1)))
+        self.across.start()
 
     def s4(self):
-        place = self.place
-
-        @pl.when(place.inner)
-        def _():
-            self.middle_back.wait_recv()
-            if place.half > 1:
-                self.give_on.start()
+        self.across.wait()
+        add_into(self.total, self.mine, self.buf, self.at + 6 * self.quarter, self.quarter)
+        self.store.start()
+
+        def both(z):
+            def work():
+                self.first_up[z].start()
+                self.first_down[z].start()
+
+            return work
+
+        self.at_z((0, self.first_up[0].start), (1, both(1)), (2, both(2)), (3, self.first_down[3].start))
 
     def s5(self):
-        place = self.place
-
-        def hop(k):
-            @pl.when(place.depth == place.half - 2 - k)
-            def _():
-                self.keep_on.wait_recv()
-                self.give_on.wait_recv()
-
-            @pl.when((place.depth == place.half - 2 - k) & place.has_out)
-            def _():
-                self.keep_on.start()
-                self.give_on.start()
-
-        hops(place.half - 1, hop)
-
-        @pl.when(place.inner)
-        def _():
-            self.middle_out.wait_send()
-            self.store.wait()
-
-        if place.half > 1:
-
-            @pl.when(jnp.logical_not(place.inner))
-            def _():
-                self.line_in.wait_send()
-
-            @pl.when(place.has_out)
-            def _():
-                self.keep_out.wait_send()
-                self.give_on.wait_send()
-
-
-KINDS = (PairFirst, LineFirst,)
-PLAN = (1, 0, 0, 0, 0, 0, 1, 1, 0, 1, 0, 0, 0, 0, 0, 1, 0, 0, 0, 0, 1, 1, 0, 1)
+        def one():
+            self.on_up[0].wait_recv()
+            self.on_up[0].start()
+            self.on_down[2].wait_recv()
+            self.on_down[2].start()
+
+        def two():
+            self.on_down[3].wait_recv()
+            self.on_down[3].start()
+            self.on_up[1].wait_recv()
+            self.on_up[1].start()
+
+        self.at_z((1, one), (2, two))
+
+    def s6(self):
+        def one():
+            self.on_down[3].wait_recv()
+            self.on_down[3].start()
+
+        def two():
+            self.on_up[0].wait_recv()
+            self.on_up[0].start()
+
+        self.at_z((1, one), (2, two))
+
+    def s7(self):
+        self.store.wait()
+
+        def zero():
+            for k in (1, 2, 3):
+                self.on_down[k].wait_recv()
+            for copy in (self.up[0], self.first_up[0]):
+                copy.wait_send()
+
+        def one():
+            for copy in (self.up[1], self.down[1], self.first_up[1], self.on_up[0]):
+                copy.wait_send()
+            for copy in (self.first_down[1], self.on_down[2], self.on_down[3]):
+                copy.wait_send()
+
+        def two():
+            for copy in (self.up[2], self.down[2], self.first_up[2], self.on_up[1], self.on_up[0]):
+                copy.wait_send()
+            for copy in (self.first_down[2], self.on_down[3]):
+                copy.wait_send()
+
+        def three():
+            for k in (0, 1, 2):
+                self.on_up[k].wait_recv()
+            for copy in (self.down[3], self.first_down[3]):
+                copy.wait_send()
+
+        self.at_z((0, zero), (1, one), (2, two), (3, three))
+
+
+KINDS = (PairFirst, LineScatter,)
+PLAN = (1, 0, 0, 1, 0, 0, 1, 0, 0, 0, 0, 0, 1, 0, 0, 0, 0, 0, 1, 1, 0, 1, 1, 0)
 TICKS = (
     (),
     (),
@@ -341,32 +366,36 @@
     (),
     (),
     (),
-    ((1, 1), (0, 1), (2, 1), (3, 1)),
-    ((6, 1),),
-    ((4, 1),),
-    (),
-    (),
-    ((5, 1), (0, 2)),
-    ((7, 1), (6, 2), (8, 1), (1, 2)),
-    ((10, 1), (2, 2), (11, 1), (3, 2)),
-    ((7, 2),),
-    ((0, 3),),
-    ((4, 2),),
-    ((1, 3),),
-    ((6, 3),),
-    (),
-    (),
-    ((2, 3), (12, 1)),
-    ((9, 1), (3, 3), (7, 3), (1, 4), (5, 2), (0, 4), (13, 1)),
-    ((8, 2), (4, 3)),
-    ((14, 1),),
-    ((2, 4), (10, 2)),
-    ((6, 4),),
-    (),
-    ((3, 4), (11, 2), (9, 2), (16, 1), (7, 4), (17, 1)),
-    ((0, 5), (15, 1)),
-    ((5, 3), (1, 5), (18, 1), (4, 4), (12, 2), (8, 3), (19, 1), (6, 5), (13, 2), (10, 3), (2, 5), (7, 5), (11, 3), (3, 5), (5, 4), (20, 1), (15, 2), (8, 4), (14, 2), (12, 3), (4, 5), (22, 1), (10, 4), (13, 3), (9, 3), (11, 4), (21, 1), (20, 2), (24, 1), (12, 4), (14, 3), (5, 5), (13, 4), (23, 1), (9, 4), (8, 5), (16, 2), (21, 2), (10, 5), (14, 4), (17, 2), (23, 2), (11, 5), (9, 5), (18, 2), (16, 3), (15, 3), (19, 2), (17, 3), (12, 5), (22, 2), (16, 4), (18, 3), (13, 5), (24, 2), (15, 4), (20, 3), (17, 4), (19, 3), (14, 5), (18, 4), (22, 3), (21, 3), (15, 5), (24, 3), (23, 3), (20, 4), (16, 5), (19, 4), (21, 4), (17, 5), (22, 4), (23, 4), (18, 5), (19, 5), (24, 4), (22, 5), (24, 5), (20, 5), (21, 5), (23, 5), (24, 6), (24, 7)),
+    ((1, 1), (0, 1), (2, 1), (3, 1), (4, 1)),
+    (),
+    ((5, 1), (6, 1)),
+    (),
+    (),
+    ((7, 1), (0, 2), (1, 2)),
+    ((3, 2), (2, 2), (8, 1), (0, 3), (6, 2), (4, 2), (9, 1)),
+    ((1, 3), (5, 2), (10, 1), (3, 3)),
+    ((6, 3), (2, 3), (7, 2)),
+    ((11, 1),),
+    (),
+    ((0, 4), (4, 3), (8, 2)),
+    (),
+    ((1, 4),),
+    (),
+    ((5, 3), (9, 2), (3, 4)),
+    ((2, 4), (6, 4), (7, 3), (10, 2), (4, 4)),
+    ((8, 3), (12, 1), (13, 1), (5, 4)),
+    (),
+    ((9, 3), (11, 2), (14, 1)),
+    (),
+    ((0, 5),),
+    ((15, 1), (7, 4), (10, 3), (18, 1), (1, 5), (8, 4)),
+    ((12, 2), (2, 5), (16, 1)),
+    ((9, 4), (19, 1), (11, 3), (3, 5), (4, 5), (17, 1), (0, 6), (6, 5), (10, 4), (5, 5), (12, 3), (18, 2), (13, 2), (19, 2), (11, 4), (3, 6), (21, 1), (6, 6), (0, 7), (14, 2), (20, 1), (7, 5), (13, 3), (18, 3), (19, 3), (8, 5), (21, 2), (22, 1), (3, 7), (6, 7), (23, 1), (14, 3), (15, 2), (13, 4), (9, 5), (22, 2), (16, 2), (21, 3), (24, 1), (10, 5), (15, 3), (17, 2), (14, 4), (22, 3), (16, 3), (20, 2), (11, 5), (12, 4), (15, 4), (17, 3), (23, 2), (16, 4), (20, 3), (18, 4), (24, 2), (13, 5), (19, 4), (12, 5), (17, 4), (23, 3), (14, 5), (21, 4), (18, 5), (20, 4), (24, 3), (15, 5), (22, 4), (19, 5), (12, 6), (16, 5), (21, 5), (23, 4), (18, 6), (17, 5), (22, 5), (19, 6), (20, 5), (21, 6), (24, 4), (22, 6), (23, 5), (12, 7), (24, 5), (18, 7), (19, 7), (21, 7), (22, 7), (24, 6), (24, 7)),
 )
+
+
+def kind_of(k, wide_count):
+    return KINDS[PLAN[k]] if wide_count == 8 else PairFirst
 
 
 def encoder(
@@ -714,7 +743,7 @@
     for layer in reversed(range(layers)):
         for row, count in spots:
             k = len(pieces)
-            kind = KINDS[PLAN[k]]
+            kind = kind_of(k, wide_count)
             piece = kind(
                 place,
                 total.at[layer],
@@ -762,7 +791,9 @@
 
     def tick():
         for k, stage in next(ticks):
-            (pieces[k][0] if k < len(pieces) else shared_piece[0]).stages[stage]()
+            stages = (pieces[k][0] if k < len(pieces) else shared_piece[0]).stages
+            if stage < len(stages):
+                stages[stage]()
 
     shared_piece = []
 
@@ -1127,7 +1158,7 @@
     shared_rows = patch + local + 64
     pieces = 12 * layers
     counts = ([hid // 4] * 8 + [cols] * 3 + [cols + 32]) * layers
-    ring_rows = sum(KINDS[kind].space(count) for kind, count in zip(PLAN, counts))
+    ring_rows = sum(kind_of(k, wide_count).space(count) for k, count in enumerate(counts))
     vmem = pl.BlockSpec(memory_space=pltpu.VMEM)
     anyw = pl.BlockSpec(memory_space=pl.ANY)
     dma = pltpu.SemaphoreType.DMA
@@ -1185,8 +1216,8 @@
         dma((8, 2)),
         dma((pieces,)),
         dma((pieces,)),
-        dma((pieces, 6)),
-        dma((pieces, 6)),
+        dma((pieces, 11)),
+        dma((pieces, 7)),
         dma((5,)),
         dma((5,)),
         dma((7,)),

time: 213 us -> 202 us (0.948)
  Pallas kernels: 212 us -> 201 us
    pallas_call x1, Pallas kernels: 203 us -> 192 us  [per_device(): pl.pallas_call(functools.partial(encoder, wide_count), out_shape=(jax.Sha...]
where the time goes in v3:
time: 202 us
  Pallas kernels  201 us (100%)
    pallas_call x1, Pallas kernels, per_device(): pl.pallas_call(functools.partial(encoder, wide_count), out_shape=(jax.Sha...  192 us
    pallas_call x1, Pallas kernels, per_device(): pl.pallas_call(widen, out_shape=(f32((local, width)), f32((local, patch))...  9.09 us

profile of v3, /device:TPU:0, one launch (start us, length us, event | category | flops | bytes accessed | tf_op | source)
XLA Modules:
  0.0 201.9 jit_solution(2238890810960900896)
XLA Ops:
  0.7 192.0 %encoder.1 = (bf16[2,2336,768]{2,1,0:T(8,128)(2,1)}, bf16[2,448,768]{2,1,0:T(8,128)(2,1)}, f32[128,768]{1,0:T(8,128)}, f32[128,256]{1,0:T(8,128)}) custom-call(bf16[128,256]{1,0:T(8,128)(2,1)} %patches_in.1, s32[1,128]{1,0:T(1,128)} %bitcast.6, bf16[128,768]{1,0:T(8,128)(2,1)} %cot_in.1, s32[2,64]{1,0:T(2,128)} %slots_in.1, bf16[512,768]{1,0:T(8,128)(2,1)} %bitcast.5, ...), custom_call_target="tpu_custom_call" | custom-call | tf_op jit(solution)/shard_map/encoder/pallas_call | solution.py:1228
  192.7 9.1 %widen.1 = (f32[128,768]{1,0:T(8,128)}, f32[128,256]{1,0:T(8,128)}, f32[2,256,768]{2,1,0:T(8,128)}, f32[2,768]{1,0:T(2,128)}, f32[768]{0:T(1024)}, /*index=5*/f3...) custom-call(bf16[2,2336,768]{2,1,0:T(8,128)(2,1)} %get-tuple-element, ...), custom_call_target="tpu_custom_call" | custom-call | tf_op jit(solution)/shard_map/widen/pallas_call | solution.py:1264

commit v4 on v3

--- a/solution.py
+++ b/solution.py
@@ -26,12 +26,17 @@
     return lax.dot_general(left, right, (((0,), (0,)), ((), ())), preferred_element_type=F32)
 
 
-def loop(count, body):
+def rolled(count, body):
     def step(index, carry):
         body(index)
         return carry
 
     lax.fori_loop(0, count, step, 0)
+
+
+def loop(count, body):
+    for index in range(count):
+        body(index)
 
 
 def hat_of(values):
@@ -63,14 +68,14 @@
 
 
 def add_into(dst, dst_row, src, src_row, rows):
-    block = next(b for b in (96, 64, 112, 48, 32, 16) if rows % b == 0)
+    block = next(b for b in (48, 32, 16) if rows % b == 0)
 
     def step(index):
         into = pl.ds(pl.multiple_of(dst_row + index * block, 16), block)
         give = pl.ds(pl.multiple_of(src_row + index * block, 16), block)
         dst[into, :] = (dst[into, :].astype(F32) + src[give, :].astype(F32)).astype(BF)
 
-    loop(rows // block, step)
+    rolled(rows // block, step)
 
 
 class Place:
@@ -100,7 +105,7 @@
     if count == 1:
         hop(0)
     elif count > 1:
-        loop(count, hop)
+        rolled(count, hop)
 
 
 class PairFirst:
@@ -355,7 +360,7 @@
 
 
 KINDS = (PairFirst, LineScatter,)
-PLAN = (1, 0, 0, 1, 0, 0, 1, 0, 0, 0, 0, 0, 1, 0, 0, 0, 0, 0, 1, 1, 0, 1, 1, 0)
+PLAN = (1, 1, 0, 0, 0, 0, 0, 1, 1, 0, 0, 0, 0, 0, 0, 1, 0, 0, 0, 0, 1, 0, 1, 0)
 TICKS = (
     (),
     (),
@@ -366,31 +371,31 @@
     (),
     (),
     (),
-    ((1, 1), (0, 1), (2, 1), (3, 1), (4, 1)),
-    (),
-    ((5, 1), (6, 1)),
+    ((0, 1),),
+    ((1, 1), (2, 1)),
     (),
     (),
-    ((7, 1), (0, 2), (1, 2)),
-    ((3, 2), (2, 2), (8, 1), (0, 3), (6, 2), (4, 2), (9, 1)),
-    ((1, 3), (5, 2), (10, 1), (3, 3)),
-    ((6, 3), (2, 3), (7, 2)),
-    ((11, 1),),
+    ((5, 1),),
+    ((4, 1), (7, 1), (2, 2), (1, 2), (3, 1), (0, 2)),
     (),
-    ((0, 4), (4, 3), (8, 2)),
+    ((8, 1), (0, 3), (1, 3), (5, 2), (2, 3)),
+    ((10, 1), (8, 2), (0, 4), (6, 1), (4, 2)),
+    ((1, 4),),
+    ((7, 2),),
+    ((5, 3), (3, 2), (8, 3), (10, 2)),
+    ((7, 3), (4, 3), (13, 1)),
     (),
-    ((1, 4),),
     (),
-    ((5, 3), (9, 2), (3, 4)),
-    ((2, 4), (6, 4), (7, 3), (10, 2), (4, 4)),
-    ((8, 3), (12, 1), (13, 1), (5, 4)),
+    ((11, 1), (5, 4), (9, 1), (1, 5), (3, 3), (0, 5), (6, 2)),
+    ((15, 1), (10, 3), (14, 1)),
+    ((6, 3), (7, 4), (11, 2)),
+    ((0, 6), (2, 4), (13, 2), (3, 4), (16, 1)),
+    ((15, 2),),
+    ((10, 4), (1, 6)),
+    ((9, 2),),
+    ((8, 4),),
+    ((11, 3), (13, 3), (12, 1), (19, 1), (20, 1), (1, 7), (7, 5), (14, 2), (9, 3), (7, 6), (22, 1), (16, 2), (4, 4), (20, 2), (0, 7), (8, 5), (12, 2), (9, 4), (14, 3), (16, 3), (23, 1), (11, 4), (19, 2), (24, 1), (15, 3), (18, 1), (13, 4), (8, 6), (4, 5), (2, 5), (20, 3), (12, 3), (24, 2), (21, 1), (22, 2), (16, 4), (14, 4), (8, 7), (19, 3), (22, 3), (23, 2), (9, 5), (17, 1), (24, 3), (6, 4), (5, 5), (11, 5), (18, 2), (23, 3), (21, 2), (16, 5), (14, 5), (17, 2), (15, 4), (10, 5), (18, 3), (21, 3), (19, 4), (24, 4), (23, 4), (20, 4), (15, 5), (17, 3), (22, 4), (20, 5), (24, 5), (6, 5), (22, 5), (21, 4), (3, 5), (18, 4), (20, 6), (7, 7), (13, 5), (22, 6), (12, 4), (17, 4), (15, 6), (23, 5), (20, 7), (24, 6), (19, 5), (12, 5), (21, 5), (22, 7), (18, 5), (24, 7), (15, 7), (17, 5)),
     (),
-    ((9, 3), (11, 2), (14, 1)),
-    (),
-    ((0, 5),),
-    ((15, 1), (7, 4), (10, 3), (18, 1), (1, 5), (8, 4)),
-    ((12, 2), (2, 5), (16, 1)),
-    ((9, 4), (19, 1), (11, 3), (3, 5), (4, 5), (17, 1), (0, 6), (6, 5), (10, 4), (5, 5), (12, 3), (18, 2), (13, 2), (19, 2), (11, 4), (3, 6), (21, 1), (6, 6), (0, 7), (14, 2), (20, 1), (7, 5), (13, 3), (18, 3), (19, 3), (8, 5), (21, 2), (22, 1), (3, 7), (6, 7), (23, 1), (14, 3), (15, 2), (13, 4), (9, 5), (22, 2), (16, 2), (21, 3), (24, 1), (10, 5), (15, 3), (17, 2), (14, 4), (22, 3), (16, 3), (20, 2), (11, 5), (12, 4), (15, 4), (17, 3), (23, 2), (16, 4), (20, 3), (18, 4), (24, 2), (13, 5), (19, 4), (12, 5), (17, 4), (23, 3), (14, 5), (21, 4), (18, 5), (20, 4), (24, 3), (15, 5), (22, 4), (19, 5), (12, 6), (16, 5), (21, 5), (23, 4), (18, 6), (17, 5), (22, 5), (19, 6), (20, 5), (21, 6), (24, 4), (22, 6), (23, 5), (12, 7), (24, 5), (18, 7), (19, 7), (21, 7), (22, 7), (24, 6), (24, 7)),
 )
 
 
@@ -446,10 +451,8 @@
     out_round,
     pre,
     mid_round,
-    grad_mixed,
     grad_qkv,
     key_acc,
-    acc,
     give,
     take,
     take_top,
@@ -507,13 +510,10 @@
     @pl.when(place.has_out)
     def _():
         pl.semaphore_signal(barrier, 1, device_id=place.outward, device_id_type=MESH)
-        pl.semaphore_wait(barrier, 6)
-
-    @pl.when(jnp.logical_not(place.has_out))
-    def _():
-        pl.semaphore_wait(barrier, 5)
 
     def span(index, size):
+        if isinstance(index, int):
+            return pl.ds(index * size, size)
         return pl.ds(pl.multiple_of(index * size, size), size)
 
     far = (w, 2 - y)
@@ -548,33 +548,41 @@
             spot = dst.at[pl.ds(h * size, size)]
             pltpu.make_async_copy(spot, spot, rows_recv.at[k, h]).wait()
 
-    send_rows(0)
-    send_rows(2)
     weights = []
     for layer in range(layers):
         for src, dst in ((att_in, wa), (comb_in, wc), (exp_in, we), (red_in, wr)):
-            weights.append((src.at[layer], dst.at[layer]))
-    own_loads = [pltpu.make_async_copy(src, dst.at[0], load_sem.at[k]) for k, (src, dst) in enumerate(weights)]
+            if dst is wc:
+                halves = [wc.at[layer, pl.ds(k * cols, cols)] for k in range(2)]
+            else:
+                halves = [dst.at[layer, k] for k in range(2)]
+            weights.append((src.at[layer], *halves))
+    own_loads = [pltpu.make_async_copy(src, own, load_sem.at[k]) for k, (src, own, _) in enumerate(weights)]
     sib_loads = [
-        Copy(src, dst.at[1], weight_send.at[k], weight_recv.at[k], sibling) for k, (src, dst) in enumerate(weights)
+        Copy(src, sib, weight_send.at[k], weight_recv.at[k], sibling) for k, (src, _, sib) in enumerate(weights)
     ]
     proj_load = pltpu.make_async_copy(proj_in, proj, load_sem.at[8])
     pos_load = pltpu.make_async_copy(pos_in, pos, load_sem.at[9])
     abias_copy = Copy(abias_in, abias.at[1], weight_send.at[8], weight_recv.at[8], sibling)
     ebias_copy = Copy(ebias_in, ebias.at[1], weight_send.at[9], weight_recv.at[9], sibling)
+    proj_load.start()
+    pos_load.start()
+    own_loads[0].start()
+
+    @pl.when(place.has_out)
+    def _():
+        pl.semaphore_wait(barrier, 6)
+
+    @pl.when(jnp.logical_not(place.has_out))
+    def _():
+        pl.semaphore_wait(barrier, 5)
+
+    send_rows(0)
+    send_rows(2)
+    sib_loads[0].start()
     abias_copy.start()
     ebias_copy.start()
-    proj_load.start()
-    pos_load.start()
-    for k in range(8):
-        own_loads[k].start()
-        sib_loads[k].start()
-        if k == 3:
-            send_rows(1)
     abias[0] = abias_in[...]
     ebias[0] = ebias_in[...]
-    small[...] = jnp.zeros_like(small)
-    bias_rows[...] = jnp.zeros_like(bias_rows)
 
     def need(k):
         own_loads[k].wait()
@@ -624,37 +632,30 @@
     offset = jnp.where(is_one > 0.5, offs_in[1:2, :].astype(F32), offs_in[0:1, :].astype(F32))
     stream[0] = jnp.where(masked > 0.5, plc_in[...].reshape(1, width).astype(F32), lifted + offset) + pos[...].astype(F32)
 
-    def before_attention(layer):
-        def norm(ch):
-            rows = span(ch, local)
-            hat, _ = hat_of(stream[layer, rows, :])
-            first[layer, rows, :] = (hat * param(scales, layer, 0) + param(shifts, layer, 0)).astype(BF)
-
-        loop(chunks, norm)
+    def norm(layer, ch):
+        rows = span(ch, local)
+        hat, _ = hat_of(stream[layer, rows, :])
+        first[layer, rows, :] = (hat * param(scales, layer, 0) + param(shifts, layer, 0)).astype(BF)
 
     def project(layer):
-        need(4 * layer)
-        if layer == 0:
-            abias_copy.wait_recv()
-            ebias_copy.wait_recv()
+        rows = slice(None)
 
         def group(g):
-            rows = first[layer]
-            query = (nt(rows, wa[layer, g, 0]) + abias[g, layer, 0:1, :].astype(F32)) * scale
-            qkv[layer, g, 0] = query.astype(BF)
-            qkv[layer, g, 1] = nt(rows, wa[layer, g, 1]).astype(BF)
-            qkv[layer, g, 2] = (nt(rows, wa[layer, g, 2]) + abias[g, layer, 1:2, :].astype(F32)).astype(BF)
+            values = first[layer, rows, :]
+            query = (nt(values, wa[layer, g, 0]) + abias[g, layer, 0:1, :].astype(F32)) * scale
+            qkv[layer, g, 0, rows, :] = query.astype(BF)
+            qkv[layer, g, 1, rows, :] = nt(values, wa[layer, g, 1]).astype(BF)
+            qkv[layer, g, 2, rows, :] = (nt(values, wa[layer, g, 2]) + abias[g, layer, 1:2, :].astype(F32)).astype(BF)
 
         loop(2, group)
 
-    def attend(layer, exchange, slot):
-        need(4 * layer + 1)
-
+    def attend(layer):
         def chunk(ch):
             rows = span(ch, local)
 
-            def group(g):
-                total_mixed = jnp.zeros((local, cols), F32)
+            groups = []
+            for g in range(2):
+                total_mixed = 0.0
                 query, key, value = qkv[layer, g, 0, rows, :], qkv[layer, g, 1], qkv[layer, g, 2]
                 for h in range(heads):
                     scores = nt(jnp.where(head_mask(local, h), query, 0), key)
@@ -662,16 +663,16 @@
                     prob = (raised / jnp.sum(raised, axis=-1, keepdims=True)).astype(BF)
                     probs[layer, g * heads + h, rows, :] = prob
                     total_mixed += nn(prob, jnp.where(head_mask(seq, h), value, 0))
-                mixed[layer, g, rows, :] = total_mixed.astype(BF)
-
-            loop(2, group)
-            offer(exchange, slot, ch, nn(mixed[layer, 0, rows, :], wc[layer, 0]) + nn(mixed[layer, 1, rows, :], wc[layer, 1]))
+                groups.append(total_mixed.astype(BF))
+            together = jnp.concatenate(groups, axis=1)
+            mixed[layer, rows, :] = together
+            offer(2 * layer, 0, ch, nn(together, wc[layer]))
 
         loop(chunks, chunk)
 
-    def to_middle(layer, exchange, slot, ch):
+    def to_middle(layer, ch):
         rows = span(ch, local)
-        values = stream[layer, rows, :] + collect(exchange, slot, ch) + cbias[layer : layer + 1, :].astype(F32)
+        values = stream[layer, rows, :] + collect(2 * layer, 0, ch) + cbias[layer : layer + 1, :].astype(F32)
         middle[layer, rows, :] = values
         hat, _ = hat_of(values)
         second[layer, rows, :] = (hat * param(scales, layer, 1) + param(shifts, layer, 1)).astype(BF)
@@ -697,47 +698,55 @@
         inner = scaled - jnp.mean(scaled, axis=-1, keepdims=True)
         return inverse * (inner - hat * jnp.mean(scaled * hat, axis=-1, keepdims=True))
 
+    for own, sib in zip(own_loads[1:], sib_loads[1:]):
+        own.start()
+        sib.start()
+    small[...] = jnp.zeros_like(small)
+    bias_rows[...] = jnp.zeros_like(bias_rows)
+
+    need(0)
+    abias_copy.wait_recv()
+    ebias_copy.wait_recv()
+    for ch in range(2):
+        norm(0, ch)
+    project(0)
     for layer in range(layers):
-        before_attention(layer)
-        project(layer)
-        attend(layer, 2 * layer, 0)
+        need(4 * layer + 1)
+        attend(layer)
         need(4 * layer + 2)
         need(4 * layer + 3)
         if layer + 1 < layers:
 
             def chunk(ch):
                 rows = span(ch, local)
-                to_middle(layer, 2 * layer, 0, ch)
-
-                def group(g):
+                to_middle(layer, ch)
+
+                part = 0.0
+                for g in range(2):
                     activate(layer, g, rows)
-                    part = nn(hidden[layer, g, rows, :], wr[layer, g])
-
-                    @pl.when(g == 0)
-                    def _():
-                        acc[...] = part
-
-                    @pl.when(g == 1)
-                    def _():
-                        acc[...] += part
-
-                loop(2, group)
-                offer(2 * layer + 1, 1, ch, acc[...])
+                    part += nn(hidden[layer, g, rows, :], wr[layer, g])
+                offer(2 * layer + 1, 1, ch, part)
 
             loop(chunks, chunk)
+            if layer == 0:
+                send_rows(1)
+            need(4 * layer + 4)
 
             def after(ch):
                 rows = span(ch, local)
                 stream[layer + 1, rows, :] = (
                     middle[layer, rows, :] + collect(2 * layer + 1, 1, ch) + rbias[layer : layer + 1, :].astype(F32)
                 )
+                norm(layer + 1, ch)
 
             loop(chunks, after)
-
+            project(layer + 1)
+
+    last = layers - 1
     pieces = []
     at = 0
     cut = hid // 4
-    spots = [(hid + (k // 2) * cut if k % 2 == 0 else (k // 2) * cut, cut) for k in range(8)]
+    spots = [(hid + k * cut if k < 4 else (k - 4) * cut, cut) for k in range(8)]
     spots += [(2 * hid + j * cols, cols) for j in range(3)] + [(2 * hid + 3 * cols, cols + 32)]
     per_layer = len(spots)
     for layer in reversed(range(layers)):
@@ -759,33 +768,43 @@
             pieces.append((piece, layer, row, count))
             at += kind.space(count)
 
-    def part_copy(k):
-        _, _, row, count = pieces[k]
+    shares = []
+    for layer in reversed(range(layers)):
+        for batch, (row, size, count) in enumerate(
+            ((hid, hid // 2, 2), (0, hid // 2, 2), (2 * hid, 3 * cols, 1), (2 * hid + 3 * cols, cols + 32, 1))
+        ):
+            shares.append((len(shares), layer, min(batch, 2), row, size, count))
+
+    def share_copy(share, u):
+        k, layer, batch, row, size, _ = share
+        slot = ((last - layer) * 3 + batch) % 2
+        start = row - (hid, 0, 2 * hid)[batch] + u * size
         return Copy(
-            send_part.at[k % 4, pl.ds(0, count)],
-            recv_part.at[pl.ds(row, count)],
-            part_send.at[k],
-            part_recv.at[k],
+            send_part.at[slot, pl.ds(start, size)],
+            recv_part.at[pl.ds(row + u * size, size)],
+            part_send.at[k, u],
+            part_recv.at[k, u],
             sibling,
         )
 
-    def begin(k, own, other):
-        _, layer, row, count = pieces[k]
-        if k >= 4:
-            part_copy(k - 4).wait_send()
-        if k == per_layer:
-            pl.semaphore_wait(credit, 1)
-        other(send_part.at[k % 4])
-        part_copy(k).start()
-        own(total.at[layer, pl.ds(row, count)])
-
-    def join(k):
-        piece, layer, row, count = pieces[k]
-        part_copy(k).wait_recv()
-        add_into(total.at[layer], row, recv_part, row, count)
-        if k == per_layer - 1:
+    def free_slot(layer, batch):
+        old = (last - layer) * 3 + batch - 2
+        for share in shares:
+            if (last - share[1]) * 3 + share[2] == old:
+                for u in range(share[5]):
+                    share_copy(share, u).wait_send()
+
+    def join(share, u):
+        k, layer, _, row, size, _ = share
+        share_copy(share, u).wait_recv()
+        start = row + u * size
+        add_into(total.at[layer], start, recv_part, start, size)
+        if k == 3:
             pl.semaphore_signal(credit, 1, device_id=sibling, device_id_type=MESH)
-        piece.stages[0]()
+        for piece, owner, spot, _ in pieces:
+            if owner == layer and start <= spot < start + size:
+                piece.stages[0]()
+                tick()
 
     ticks = iter(TICKS)
 
@@ -797,47 +816,58 @@
 
     shared_piece = []
 
-    def weight_grad(left, right):
-        def into(ref):
-            ref[pl.ds(0, left.shape[1]), :] = tn(left[...], right[...]).astype(BF)
-
-        return into
-
-    def run_pieces(base, works):
-        for i, (own, other) in enumerate(works):
-            begin(base + i, own, other)
-            if i > 0:
-                join(base + i - 1)
-                tick()
-        join(base + len(works) - 1)
-        tick()
-
-    def feed_grads(layer, base):
-        works = []
-        for k in range(8):
-            lanes = pl.ds((k // 2) * cut, cut)
-            if k % 2 == 0:
-                works.append([weight_grad(hidden.at[layer, g, :, lanes], out_round) for g in range(2)])
-            else:
-                works.append([weight_grad(second.at[layer, :, lanes], pre.at[g]) for g in range(2)])
-        run_pieces(base, works)
-
-    def attention_grads(layer, base):
-        def comb(g):
-            grad_comb = weight_grad(mixed.at[layer, g], mid_round)
-
-            def into(ref):
-                grad_comb(ref)
-                ref[pl.ds(cols, 32), :] = bias_rows[layer, g].astype(BF)
-
-            return into
-
-        works = [[weight_grad(grad_qkv.at[g, j], first.at[layer]) for g in range(2)] for j in range(3)]
-        works.append([comb(g) for g in range(2)])
-        run_pieces(base + 8, works)
+    def feed_grads(layer, batch):
+        share = shares[4 * (last - layer) + batch]
+        row = share[3]
+        slot = ((last - layer) * 3 + batch) % 2
+        free_slot(layer, batch)
+        if layer < last and batch == 0:
+            pl.semaphore_wait(credit, 1)
+
+        def half(u):
+            def block(t):
+                lanes = pl.ds(pl.multiple_of((u * (hid // 256) + t) * 128, 128), 128)
+                into = pl.ds(pl.multiple_of((u * (hid // 256) + t) * 128, 128), 128)
+                for g in (1, 0):
+                    if batch == 0:
+                        values = tn(hidden[layer, g, :, lanes], out_round[...])
+                    else:
+                        values = tn(second[layer, :, lanes], pre[g])
+                    if g == 1:
+                        send_part[slot, into, :] = values.astype(BF)
+                    else:
+                        total[layer, pl.ds(row + into.start, 128), :] = values.astype(BF)
+
+            rolled(hid // 256, block)
+            share_copy(share, u).start()
+
+        rolled(2, half)
+        for u in range(2):
+            join(share, u)
+
+    def attention_grads(layer):
+        three, one = shares[4 * (last - layer) + 2], shares[4 * (last - layer) + 3]
+        slot = ((last - layer) * 3 + 2) % 2
+        row = 2 * hid
+        free_slot(layer, 2)
+
+        def block(j):
+            into = pl.ds(pl.multiple_of(j * cols, 16), cols)
+            send_part[slot, into, :] = tn(grad_qkv[1, j], first[layer]).astype(BF)
+            total[layer, pl.ds(row + into.start, cols), :] = tn(grad_qkv[0, j], first[layer]).astype(BF)
+
+        rolled(3, block)
+        share_copy(three, 0).start()
+        both = tn(mixed[layer], mid_round[...])
+        send_part[slot, pl.ds(3 * cols, cols), :] = both[cols:].astype(BF)
+        send_part[slot, pl.ds(4 * cols, 32), :] = bias_rows[layer, 1].astype(BF)
+        share_copy(one, 0).start()
+        total[layer, pl.ds(row + 3 * cols, cols), :] = both[:cols].astype(BF)
+        total[layer, pl.ds(row + 4 * cols, 32), :] = bias_rows[layer, 0].astype(BF)
+        join(three, 0)
+        join(one, 0)
 
     wait_rows(1, cot, local)
-    last = layers - 1
 
     def start_back(ch):
         rows = span(ch, local)
@@ -851,7 +881,6 @@
     top_copy = Copy(give.at[2], take_top, last_send.at[1], last_recv.at[1], partner)
 
     for layer in reversed(range(layers)):
-        base = (last - layer) * per_layer
         exchange = 4 + 2 * (last - layer)
 
         def chunk(ch):
@@ -859,24 +888,13 @@
             note(10 + layer, grad[rows, :])
             out_round[rows, :] = grad[rows, :].astype(BF)
             if layer == last:
-                to_middle(layer, 2 * layer, 0, ch)
-
-            def group(g):
-                if layer == last:
-                    activate(layer, g, rows)
+                to_middle(layer, ch)
+                loop(2, lambda g: activate(layer, g, rows))
+            part = 0.0
+            for g in range(2):
                 feed_back(layer, g, rows)
-                part = nt(pre[g, rows, :], we[layer, g])
-
-                @pl.when(g == 0)
-                def _():
-                    acc[...] = part
-
-                @pl.when(g == 1)
-                def _():
-                    acc[...] += part
-
-            loop(2, group)
-            offer(exchange, 1, ch, acc[...])
+                part += nt(pre[g, rows, :], we[layer, g])
+            offer(exchange, 1, ch, part)
 
         loop(chunks, chunk)
         tick()
@@ -895,7 +913,8 @@
             def _():
                 top_copy.start()
 
-        feed_grads(layer, base)
+        feed_grads(layer, 0)
+        feed_grads(layer, 1)
 
         def chunk(ch):
             rows = span(ch, local)
@@ -906,11 +925,9 @@
             mid_round[rows, :] = grad_middle.astype(BF)
 
             def group(g):
-                mixed_back = nt(mid_round[rows, :], wc[layer, g]).astype(BF)
+                mixed_back = nt(mid_round[rows, :], wc[layer, span(g, cols), :]).astype(BF)
                 query, key, value = qkv[layer, g, 0, rows, :], qkv[layer, g, 1], qkv[layer, g, 2]
-                query_acc = jnp.zeros((local, cols), F32)
-                key_sum = jnp.zeros((seq, cols), F32)
-                value_sum = jnp.zeros((seq, cols), F32)
+                query_acc, key_sum, value_sum = 0.0, 0.0, 0.0
                 for h in range(heads):
                     prob = probs[layer, g * heads + h, rows, :]
                     back = jnp.where(head_mask(local, h), mixed_back, 0)
@@ -925,13 +942,10 @@
                 grad_qkv[g, 0, rows, :] = grad_query
                 bias_rows[layer, g, 1:2, 0:cols] += column_sums(grad_query.astype(F32))
 
-                @pl.when(ch == 0)
-                def _():
+                if ch == 0:
                     key_acc[g, 0] = key_sum
                     key_acc[g, 1] = value_sum
-
-                @pl.when(ch > 0)
-                def _():
+                else:
                     key_acc[g, 0] += key_sum
                     key_acc[g, 1] += value_sum
 
@@ -951,27 +965,15 @@
         def chunk(ch):
             rows = span(ch, local)
 
-            def group(g):
-                part = (
-                    nn(grad_qkv[g, 0, rows, :], wa[layer, g, 0])
-                    + nn(grad_qkv[g, 1, rows, :], wa[layer, g, 1])
-                    + nn(grad_qkv[g, 2, rows, :], wa[layer, g, 2])
-                )
-
-                @pl.when(g == 0)
-                def _():
-                    acc[...] = part
-
-                @pl.when(g == 1)
-                def _():
-                    acc[...] += part
-
-            loop(2, group)
-            offer(exchange + 1, 0, ch, acc[...])
+            part = 0.0
+            for g in range(2):
+                for j in range(3):
+                    part += nn(grad_qkv[g, j, rows, :], wa[layer, g, j])
+            offer(exchange + 1, 0, ch, part)
 
         loop(chunks, chunk)
         tick()
-        attention_grads(layer, base)
+        attention_grads(layer)
 
         if layer == last:
 
@@ -1123,8 +1125,8 @@
 
     for copy in sib_loads + [abias_copy, ebias_copy]:
         copy.wait_send()
-    for k in range(count - 4, count):
-        part_copy(k).wait_send()
+    free_slot(-1, 0)
+    free_slot(-1, 1)
 
 
 def per_device(
@@ -1164,7 +1166,7 @@
     dma = pltpu.SemaphoreType.DMA
     scratch = [
         pltpu.VMEM((layers, 2, 3, cols, width), BF),
-        pltpu.VMEM((layers, 2, cols, width), BF),
+        pltpu.VMEM((layers, 2 * cols, width), BF),
         pltpu.VMEM((layers, 2, width, hid), BF),
         pltpu.VMEM((layers, 2, hid, width), BF),
         pltpu.VMEM((2, layers, 2, cols), BF),
@@ -1181,21 +1183,19 @@
         pltpu.VMEM((layers, seq, width), BF),
         pltpu.VMEM((layers, 2, 3, seq, cols), BF),
         pltpu.VMEM((layers, 2 * heads, seq, seq), BF),
-        pltpu.VMEM((layers, 2, seq, cols), BF),
+        pltpu.VMEM((layers, seq, 2 * cols), BF),
         pltpu.VMEM((layers, 2, seq, hid), BF),
         pltpu.VMEM((layers, 2, seq, hid), BF),
         pltpu.VMEM((seq, width), BF),
         pltpu.VMEM((2, seq, hid), BF),
         pltpu.VMEM((seq, width), BF),
-        pltpu.VMEM((8, 128), BF),
         pltpu.VMEM((2, 3, seq, cols), BF),
         pltpu.VMEM((2, 2, seq, cols), F32),
-        pltpu.VMEM((local, width), F32),
         pltpu.VMEM((3, seq, width), BF),
         pltpu.VMEM((2, seq, width), BF),
         pltpu.VMEM((seq, width), BF),
         pltpu.VMEM((seq, width), BF),
-        pltpu.VMEM((4, cols + 32, width), BF),
+        pltpu.VMEM((2, 4 * cols + 32, width), BF),
         pltpu.VMEM((per_layer, width), BF),
         pltpu.VMEM((layers, per_layer, width), BF),
         pltpu.VMEM((ring_rows, width), BF),
@@ -1214,8 +1214,8 @@
         dma((3, 2)),
         dma((8, 2)),
         dma((8, 2)),
-        dma((pieces,)),
-        dma((pieces,)),
+        dma((4 * layers, 2)),
+        dma((4 * layers, 2)),
         dma((pieces, 11)),
         dma((pieces, 7)),
         dma((5,)),
@@ -1290,8 +1290,8 @@
             pltpu.VMEM((2, patch + local, width), F32),
             pltpu.VMEM((local, width), F32),
             pltpu.VMEM((local, patch), F32),
-            dma((layers, 4)),
-            dma((layers, 6)),
+            dma((layers, 8)),
+            dma((layers, 8)),
             dma((2,)),
             dma((2, 2)),
             dma((2, 2)),
@@ -1345,11 +1345,15 @@
             ((encoded, encoded_held, encoded_out), (grad_patches, patches_held, patches_out))
         )
     ]
-    tail = sums.shape[1] - 3 * cols - 2 * hid
-    cuts = ((0, hid), (hid, hid), (2 * hid, 3 * cols), (2 * hid + 3 * cols, tail))
+    half = hid // 2
+    cuts = []
+    for k, array in enumerate((expander, reducer)):
+        cuts += [(k * hid + u * half, half, array, u) for u in range(2)]
+    cuts += [(2 * hid + j * cols, cols, attention, j) for j in range(3)]
+    cuts.append((2 * hid + 3 * cols, sums.shape[1] - 3 * cols - 2 * hid, combiner, 0))
     loads = []
     for layer in range(layers):
-        for k, (row, count) in enumerate(cuts):
+        for k, (row, count, _, _) in enumerate(cuts):
             spot = (layer, pl.ds(row, count))
             loads.append(pltpu.make_async_copy(sums.at[spot], sums_in.at[spot], load_sem.at[layer, k]))
     shared_loads = [pltpu.make_async_copy(shared.at[k], shared_in.at[k], shared_sem.at[k]) for k in range(2)]
@@ -1362,21 +1366,17 @@
             rows = pl.ds(pl.multiple_of(row + t * 64, 64), 64)
             dst[rows, :] = src[rows, :].astype(F32)
 
-        loop(count // 64, step)
+        rolled(count // 64, step)
 
     for layer in range(layers):
-        for k, (row, count) in enumerate(cuts):
+        for k, (row, count, array, u) in enumerate(cuts):
             loads[layer * len(cuts) + k].wait()
             wide = min(count, sums_wide.shape[1] - row)
             convert(sums_in.at[layer], sums_wide.at[layer], row, wide)
-            if k == 2:
-                targets = [(attention.at[layer, j], row + j * cols, cols, 2 + j) for j in range(3)]
-            else:
-                targets = [((expander, reducer, None, combiner)[k].at[layer], row, wide, (0, 1, None, 5)[k])]
-            for target, start, size, sem in targets:
-                copy = pltpu.make_async_copy(sums_wide.at[layer, pl.ds(start, size)], target, store_sem.at[layer, sem])
-                copy.start()
-                stores.append(copy)
+            target = array.at[layer, u] if array is attention else array.at[layer, pl.ds(u * half, wide)]
+            copy = pltpu.make_async_copy(sums_wide.at[layer, pl.ds(row, wide)], target, store_sem.at[layer, k])
+            copy.start()
+            stores.append(copy)
         bias = sums_in[layer, pl.ds(2 * hid + 4 * cols, 16), :].astype(F32)
         expand_bias[layer : layer + 1, :] = bias[0:1, :]
         attn_bias[layer, 0:1, :] = bias[1:2, :cols]

time: 202 us -> 197 us (0.975)
  Pallas kernels: 201 us -> 196 us
    pallas_call x1, Pallas kernels: 192 us -> 186 us  [per_device(): pl.pallas_call(functools.partial(encoder, wide_count), out_shape=(jax.Sha...]
where the time goes in v4:
time: 197 us; the launch traced here: 196 us
  Pallas kernels  196 us (99%)
    pallas_call x1, Pallas kernels, per_device(): pl.pallas_call(functools.partial(encoder, wide_count), out_shape=(jax.Sha...  186 us
    pallas_call x1, Pallas kernels, per_device(): pl.pallas_call(widen, out_shape=(f32((local, width)), f32((local, patch))...  9.27 us

profile of v4, /device:TPU:0, one launch (start us, length us, event | category | flops | bytes accessed | tf_op | source)
XLA Modules:
  0.0 196.5 jit_solution(8432084703669090703)
XLA Ops:
  0.7 186.4 %encoder.1 = (bf16[2,2336,768]{2,1,0:T(8,128)(2,1)}, bf16[2,448,768]{2,1,0:T(8,128)(2,1)}, f32[128,768]{1,0:T(8,128)}, f32[128,256]{1,0:T(8,128)}) custom-call(bf16[128,256]{1,0:T(8,128)(2,1)} %patches_in.1, s32[1,128]{1,0:T(1,128)} %bitcast.6, bf16[128,768]{1,0:T(8,128)(2,1)} %cot_in.1, s32[2,64]{1,0:T(2,128)} %slots_in.1, bf16[512,768]{1,0:T(8,128)(2,1)} %bitcast.5, ...), custom_call_target="tpu_custom_call" | custom-call | tf_op jit(solution)/shard_map/encoder/pallas_call | solution.py:1228
  187.0 9.3 %widen.1 = (f32[128,768]{1,0:T(8,128)}, f32[128,256]{1,0:T(8,128)}, f32[2,256,768]{2,1,0:T(8,128)}, f32[2,768]{1,0:T(2,128)}, f32[768]{0:T(1024)}, /*index=5*/f3...) custom-call(bf16[2,2336,768]{2,1,0:T(8,128)(2,1)} %get-tuple-element, ...), custom_call_target="tpu_custom_call" | custom-call | tf_op jit(solution)/shard_map/widen/pallas_call | solution.py:1264

commit v5 on v4

--- a/solution.py
+++ b/solution.py
@@ -1092,10 +1092,9 @@
 
     sum_shared.stages = sum_shared.stages[:5] + [to_partner, to_sibling, close_shared]
     shared_piece.append(sum_shared)
+    count = len(pieces)
     sum_shared.s0()
     tick()
-    tick()
-    count = len(pieces)
 
     @pl.when(diagonal)
     def _():
@@ -1113,6 +1112,8 @@
     )
     for copy in finals:
         copy.start()
+    tick()
+
     for copy in finals:
         copy.wait()
 

time: 197 us -> 197 us (level)
  no operation moved by 1% of the time
where the time goes in v5:
time: 197 us; the launch traced here: 196 us
  Pallas kernels  196 us (99%)
    pallas_call x1, Pallas kernels, per_device(): pl.pallas_call(functools.partial(encoder, wide_count), out_shape=(jax.Sha...  186 us
    pallas_call x1, Pallas kernels, per_device(): pl.pallas_call(widen, out_shape=(f32((local, width)), f32((local, patch))...  9.27 us

profile of v5, /device:TPU:0, one launch (start us, length us, event | category | flops | bytes accessed | tf_op | source)
XLA Modules:
  0.0 196.5 jit_solution(8432084703669090703)
XLA Ops:
  0.7 186.4 %encoder.1 = (bf16[2,2336,768]{2,1,0:T(8,128)(2,1)}, bf16[2,448,768]{2,1,0:T(8,128)(2,1)}, f32[128,768]{1,0:T(8,128)}, f32[128,256]{1,0:T(8,128)}) custom-call(bf16[128,256]{1,0:T(8,128)(2,1)} %patches_in.1, s32[1,128]{1,0:T(1,128)} %bitcast.6, bf16[128,768]{1,0:T(8,128)(2,1)} %cot_in.1, s32[2,64]{1,0:T(2,128)} %slots_in.1, bf16[512,768]{1,0:T(8,128)(2,1)} %bitcast.5, ...), custom_call_target="tpu_custom_call" | custom-call | tf_op jit(solution)/shard_map/encoder/pallas_call | solution.py:1229
  187.0 9.3 %widen.1 = (f32[128,768]{1,0:T(8,128)}, f32[128,256]{1,0:T(8,128)}, f32[2,256,768]{2,1,0:T(8,128)}, f32[2,768]{1,0:T(2,128)}, f32[768]{0:T(1024)}, /*index=5*/f3...) custom-call(bf16[2,2336,768]{2,1,0:T(8,128)(2,1)} %get-tuple-element, ...), custom_call_target="tpu_custom_call" | custom-call | tf_op jit(solution)/shard_map/widen/pallas_call | solution.py:1265
